TPU v7x, 128 devices: a whole 4x4x4 slice. The times are simulated.
128 devices in a mesh: row: 8 (over x, z_hi), col: 16 (over z_lo, y, core).
Axes of the slice: x: 4, y: 4, z: 4 (z_hi: 2, z_lo: 2; z = z_hi * 2 + z_lo), core: 2. Of those that a mesh axis runs over, the one named last changes fastest.
Arguments:
- amplitudes: bfloat16 [800, 800, 768], P('row', 'col'), may hold values from -6 to 6
- integrals: bfloat16 [800, 800, 1024], P('row', 'col'), may hold values from -0.1875 to 0.1875
- window_index: int32 [1024], replicated, may hold values from 0 to 639999, as said below
Outputs:
- residual: bfloat16 [800, 800, 768], P('row', 'col')
- pair_energy: float32 [768], replicated
Inputs may be any that keep to these rules, and one draw needn't show every extreme that they name: `window_index`: the window pairs are distinct; pair k lies in the block of a rows and b columns owned by device number k // 8 in row-major order of the (a, b) device grid, 8 pairs for each block.
All inputs are finite; a program needn't handle non-finite values.
Results may differ from a plain program's by a relative error of at most 0.001.
Values may be sent and summed in bfloat16 or wider, within the bound.
No kernel may reach another device: no remote copies, remote signals or barrier semaphores. Data moves between devices by JAX's collectives and lax.ppermute only.
A program may use at most 128 MiB of HBM per device.

v0:
```python
import functools

import jax
import jax.numpy as jnp
from jax import lax
from jax.sharding import Mesh
from jax.sharding import PartitionSpec as P

COL = ("col_0", "col_1", "col_2")
ROW = ("row_0", "row_1")
ROW_COL = ("row_0", "row_1", "col_0", "col_1", "col_2")


def copy_for_each(array, axis):
    devices = lax.axis_size(axis)
    return lax.all_to_all(
        jnp.broadcast_to(array[None], (devices, *array.shape)), axis, 0, 0, tiled=True
    )


def laid_out(pieces, dim):
    pieces = jnp.moveaxis(pieces, 0, dim)
    shape = pieces.shape
    return pieces.reshape(*shape[:dim], shape[dim] * shape[dim + 1], *shape[dim + 2 :])


def collect(array, axis, dim):
    pieces = copy_for_each(array, axis)
    return laid_out(pieces, dim)


def one_axis_at_a_time(array, axes):
    return functools.reduce(lax.psum, axes, array)


def shards(amplitudes, integrals, window_index):
    block_rows, block_cols, pairs = amplitudes.shape
    window = integrals.shape[2]
    ncols = lax.axis_size(COL)
    nrows = lax.axis_size(ROW)
    per_device = window // (nrows * ncols)
    row_rank = lax.axis_index(ROW)
    col_rank = lax.axis_index(COL)
    linear_rank = row_rank * ncols + col_rank
    owned_index = lax.dynamic_slice_in_dim(window_index, linear_rank * per_device, per_device)
    virtuals = block_rows * nrows
    row_offset = owned_index // virtuals - row_rank * block_rows
    col_offset = owned_index % virtuals - col_rank * block_cols
    owned = amplitudes[row_offset, col_offset]
    in_row = collect(owned, COL, 0)
    columns = collect(in_row, ROW, 0)
    full = jnp.einsum("abk,kp->abp", integrals, columns, preferred_element_type=jnp.float32)
    partial_value = jnp.sum(amplitudes.astype(jnp.float32) * full, axis=(0, 1))
    pair_energy = one_axis_at_a_time(partial_value, ROW_COL) / virtuals
    residual = full.astype(jnp.bfloat16)
    return (residual, pair_energy)


def solution(mesh):
    finer = Mesh(mesh.devices.reshape(4, 2, 2, 4, 2), ("row_0", "row_1", "col_0", "col_1", "col_2"))
    placed = (P(ROW, COL, None), P(ROW, COL, None), P())
    return jax.shard_map(
        shards, mesh=finer, in_specs=placed, out_specs=(P(ROW, COL, None), P()), check_vma=False
    )
```

profile of v0, /device:TPU:0, one launch (start us, length us, event | category | flops | bytes accessed | tf_op | source)
XLA Modules:
  0.0 101.4 jit_solution(7970798104723668916)
XLA Ops:
  0.6 0.8 fusion.4
  1.4 1.4 %gather_fusion = bf16[8,768]{1,0:T(8,128)(2,1)S(1)} fusion(bf16[100,50,768]{2,0,1:T(8,128)(2,1)} %param.3, s32[8]{0:T(128)S(1)} %fusion.4), kind=kCustom, calls=%fused_computation | custom fusion | bytes 24640 | tf_op jit(solution)/shard_map/gather | solution.py:49
  2.8 12.9 %all_to_all.10 = bf16[16,8,768]{2,1,0:T(8,128)(2,1)S(1)} all-to-all(bf16[16,8,768]{2,1,0:T(8,128)(2,1)S(1)} %broadcast_in_dim.21), channel_id=1, replica_groups=mesh['row_0'=4,'row_1'=2,'col_0'=2,'col_1'=4,'col_2'=2] {'col_0','col_1'..., dimensions={0} | all-to-all | bytes 393216 | tf_op jit(solution)/shard_map/all_to_all | solution.py:16
  15.7 0.1 broadcast_in_dim.23
  15.8 0.0 slice-start
  15.9 30.0 %all_to_all.11 = bf16[8,128,768]{2,1,0:T(8,128)(2,1)S(1)} all-to-all(bf16[8,128,768]{2,1,0:T(8,128)(2,1)S(1)} %broadcast_in_dim.23), channel_id=1, replica_groups=mesh['row_0'=4,'row_1'=2,'col_0'=2,'col_1'=4,'col_2'=2] {'row_0','row_1'}, dimensions={0} | all-to-all | bytes 3145728 | tf_op jit(solution)/shard_map/all_to_all | solution.py:16
  45.8 0.0 slice-start.1
  45.8 16.5 %bitcast_convert_fusion = (bf16[100,50,768]{2,0,1:T(8,128)(2,1)}, f32[768,100,50]{0,1,2:T(8,128)}) fusion(bf16[1024,768,1]{1,0,2:T(8,128)(2,1)S(1)} %bitcast.13, bf16[100,50,1024]{2,0,1:T(8,128)(2,1)} %param.4), kind=kOutput, calls=%fused_computation.2 | convolution fusion | flops 7868160000 | bytes 34852864 | tf_op jit(solution)/shard_map/abk,kp->abp/dot_general | solution.py:52
  62.4 0.0 slice-done
  62.4 0.0 slice-done.1
  62.4 6.8 %fusion = f32[768]{0:T(1024)S(1)} fusion(f32[768,100,50]{0,1,2:T(8,128)} %get-tuple-element.3, bf16[100,50,768]{2,0,1:T(8,128)(2,1)S(1)} %bitcast.12), kind=kLoop, calls=%fused_computation.3 | loop fusion | flops 11519232 | bytes 23043072 | tf_op jit(solution)/shard_map/reduce_sum | solution.py:53
  69.2 9.0 %psum.35 = f32[768]{0:T(1024)S(1)} all-reduce(f32[768]{0:T(1024)S(1)} %fusion), channel_id=1, replica_groups=mesh['row_0'=4,'row_1'=2,'col_0'=2,'col_1'=4,'col_2'=2] {'row_0'}, use_global_device_ids=true, to_apply=%region_1.2 | all-reduce | flops 768 | bytes 6144 | tf_op jit(solution)/shard_map/psum | solution.py:33
  78.2 6.4 %psum.36 = f32[768]{0:T(1024)S(1)} all-reduce(f32[768]{0:T(1024)S(1)} %psum.35), channel_id=1, replica_groups=mesh['row_0'=4,'row_1'=2,'col_0'=2,'col_1'=4,'col_2'=2] {'row_1'}, use_global_device_ids=true, to_apply=%region_2.3 | all-reduce | flops 768 | bytes 6144 | tf_op jit(solution)/shard_map/psum | solution.py:33
  84.6 4.9 %psum.37 = f32[768]{0:T(1024)S(1)} all-reduce(f32[768]{0:T(1024)S(1)} %psum.36), channel_id=1, replica_groups=mesh['row_0'=4,'row_1'=2,'col_0'=2,'col_1'=4,'col_2'=2] {'col_0'}, use_global_device_ids=true, to_apply=%region_3.4 | all-reduce | flops 768 | bytes 6144 | tf_op jit(solution)/shard_map/psum | solution.py:33
  89.5 8.8 %psum.38 = f32[768]{0:T(1024)S(1)} all-reduce(f32[768]{0:T(1024)S(1)} %psum.37), channel_id=1, replica_groups=mesh['row_0'=4,'row_1'=2,'col_0'=2,'col_1'=4,'col_2'=2] {'col_1'}, use_global_device_ids=true, to_apply=%region_4.5 | all-reduce | flops 768 | bytes 6144 | tf_op jit(solution)/shard_map/psum | solution.py:33
  98.3 2.5 %psum.39 = f32[768]{0:T(1024)S(1)} all-reduce(f32[768]{0:T(1024)S(1)} %psum.38), channel_id=1, replica_groups=mesh['row_0'=4,'row_1'=2,'col_0'=2,'col_1'=4,'col_2'=2] {'col_2'}, use_global_device_ids=true, to_apply=%region_5.6 | all-reduce | flops 768 | bytes 6144 | tf_op jit(solution)/shard_map/psum | solution.py:33
  100.8 0.6 broadcast_multiply_fusion
  (2 shorter events, 0.0 us)
Async XLA Ops:
  15.8 46.5 %slice-start = ((s8[7987200]{0:T(1024)(128)(4,1)}), s8[4194304]{0:T(1024)(128)(4,1)S(1)}, s32[]{:S(2)}) async-start(s8[7987200]{0:T(1024)(128)(4,1)} %bitcast.11), calls=%async_computation.2 | async-start | bytes 8388608
  45.8 16.5 %slice-start.1 = ((s8[7987200]{0:T(1024)(128)(4,1)}), s8[3792896]{0:T(1024)(128)(4,1)S(1)}, s32[]{:S(2)}) async-start(s8[7987200]{0:T(1024)(128)(4,1)} %bitcast.11), calls=%async_computation.3 | async-start | bytes 7585792
where the time goes:
time: 103 us; the launch traced here: 101 us
  blocking collectives  74.5 us (72%)
  matrix products  16.5 us (16%)
  other arithmetic  8.16 us (8%)
  local copies, waits for them, and re-layouts  1.5 us (1%)
    all_to_all x2, blocking collectives, copy_for_each(): lax.all_to_all(jnp.broadcast_to(array[None], (devices, *array.shape)), ax...  42.9 us
    psum x5, blocking collectives, one_axis_at_a_time(): return functools.reduce(lax.psum, axes, array)  31.6 us
    dot_general x1, matrix products, shards(): jnp.einsum('abk,kp->abp', integrals, columns, preferred_element_type=jnp....  16.5 us
    reduce_sum x1, other arithmetic, shards(): partial_value = jnp.sum(amplitudes.astype(jnp.float32) * full, axis=(0, 1))  6.78 us

commit v1 on v0

v1 whole, which is shorter than its diff:
```python
import functools

import jax
import jax.numpy as jnp
from jax import lax
from jax.experimental import pallas as pl
from jax.experimental.pallas import tpu as pltpu
from jax.sharding import Mesh
from jax.sharding import PartitionSpec as P

AXES = ("x", "zh", "zl", "y", "c")
ROW = ("x", "zh")
COL = ("zl", "y", "c")
CHIPS = ("x", "zh", "zl", "y")
SWAP = [(0, 1), (1, 0)]
STEP_COLS = 10


def share(array, axes):
    devices = lax.axis_size(axes)
    return lax.all_to_all(
        jnp.broadcast_to(array[None], (devices, *array.shape)), axes, 0, 0, tiled=True
    )


def ladder_kernel(core_ref, own_ref, other_ref, ints_ref, amps_ref, res_ref, energy_ref, cols_ref, sum_ref):
    step = pl.program_id(0)
    nb, rows, window = ints_ref.shape

    @pl.when(step == 0)
    def _():
        core = core_ref[0]
        cols_ref[:, core] = own_ref[...]
        cols_ref[:, 1 - core] = other_ref[...]
        sum_ref[...] = jnp.zeros_like(sum_ref)

    pad = -rows % 8
    whole = rows // 8 * 8

    def padded(block):
        if pad == 0:
            return block
        return jnp.concatenate([block, jnp.zeros((pad, window), block.dtype)], 0)

    lhs = jnp.concatenate([padded(ints_ref[j]) for j in range(nb)], 0)
    cols = cols_ref[...].reshape(window, -1)
    full = jnp.dot(lhs, cols, preferred_element_type=jnp.float32)
    for j in range(nb):
        part = full[j * (rows + pad) : j * (rows + pad) + rows]
        res_ref[j] = part.astype(res_ref.dtype)
        product = amps_ref[j].astype(jnp.float32) * part
        sum_ref[...] += jnp.sum(product[:whole].reshape(whole // 8, 8, -1), 0)
        if rows > whole:
            sum_ref[: rows - whole] += product[whole:]

    @pl.when(step == pl.num_programs(0) - 1)
    def _():
        energy_ref[...] = jnp.sum(sum_ref[...], 0, keepdims=True)


def ladder(core, own, other, ints, amps):
    blocks, rows, window = ints.shape
    pairs = amps.shape[2]
    nb = STEP_COLS
    moving = lambda s, c: (s, 0, 0)
    still = lambda s, c: (0, 0, 0)
    return pl.pallas_call(
        ladder_kernel,
        out_shape=(
            jax.ShapeDtypeStruct(amps.shape, jnp.bfloat16),
            jax.ShapeDtypeStruct((1, pairs), jnp.float32),
        ),
        grid_spec=pltpu.PrefetchScalarGridSpec(
            num_scalar_prefetch=1,
            grid=(blocks // nb,),
            in_specs=[
                pl.BlockSpec(own.shape, still),
                pl.BlockSpec(other.shape, still),
                pl.BlockSpec((nb, rows, window), moving),
                pl.BlockSpec((nb, rows, pairs), moving),
            ],
            out_specs=[
                pl.BlockSpec((nb, rows, pairs), moving),
                pl.BlockSpec((1, pairs), lambda s, c: (0, 0)),
            ],
            scratch_shapes=[
                pltpu.VMEM((own.shape[0], 2, own.shape[1], pairs), own.dtype),
                pltpu.VMEM((8, pairs), jnp.float32),
            ],
        ),
        compiler_params=pltpu.CompilerParams(
            vmem_limit_bytes=48 << 20, dimension_semantics=("arbitrary",)
        ),
        cost_estimate=pl.CostEstimate(
            flops=2 * blocks * rows * window * pairs,
            bytes_accessed=2 * blocks * rows * (window + 2 * pairs),
            transcendentals=0,
        ),
    )(core, own, other, ints, amps)


def shards(amplitudes, integrals, window_index):
    block_rows, block_cols, pairs = amplitudes.shape
    window = integrals.shape[2]
    per_device = window // lax.axis_size(AXES)
    row_rank = lax.axis_index(ROW)
    col_rank = lax.axis_index(COL)
    virtuals = block_rows * lax.axis_size(ROW)
    owned_index = lax.dynamic_slice_in_dim(window_index, lax.axis_index(AXES) * per_device, per_device)
    row_offset = owned_index // virtuals - row_rank * block_rows
    col_offset = owned_index % virtuals - col_rank * block_cols
    owned = amplitudes[row_offset, col_offset]
    line = share(owned, ("y",)).reshape(-1, pairs)
    own = share(line, ("x", "zh", "zl")).reshape(-1, per_device, pairs)
    other = lax.ppermute(own, "c", SWAP)
    core = lax.axis_index("c").reshape(1)
    residual, energy = ladder(
        core, own, other, integrals.transpose(1, 0, 2), amplitudes.transpose(1, 0, 2)
    )
    chip = energy + lax.ppermute(energy, "c", SWAP)
    total = jnp.sum(share(chip, CHIPS), axis=(0, 1))
    return residual.transpose(1, 0, 2), total / virtuals


def solution(mesh):
    finer = Mesh(mesh.devices.reshape(4, 2, 2, 4, 2), AXES)
    placed = (P(ROW, COL, None), P(ROW, COL, None), P())
    return jax.shard_map(
        shards, mesh=finer, in_specs=placed, out_specs=(P(ROW, COL, None), P()), check_vma=False
    )
```

time: 103 us -> 67.3 us (0.65); the launches traced: 101 us -> 67 us
  blocking collectives: 74.5 us -> 45.6 us
  matrix products: 16.5 us -> 0 us
  Pallas kernels: 0 us -> 14.3 us
  other arithmetic: 8.16 us -> 1.54 us
  waiting for transfers between devices: 0 us -> 3.31 us
    psum x5 -> x0, blocking collectives: 31.6 us -> none  [one_axis_at_a_time(): return functools.reduce(lax.psum, axes, array)]
    dot_general x1 -> x0, matrix products: 16.5 us -> none  [shards(): jnp.einsum('abk,kp->abp', integrals, columns, preferred_element_type=jnp....]
    pallas_call x0 -> x1, Pallas kernels: none -> 14.3 us  [ladder(): pl.pallas_call(ladder_kernel, out_shape=(jax.ShapeDtypeStruct(amps.shape,...]
    reduce_sum x1, other arithmetic: 6.78 us -> 0.15 us  [shards(): total = jnp.sum(share(chip, CHIPS), axis=(0, 1))]
    ppermute x0 -> x2, waiting for transfers between devices: none -> 3.31 us  [the longest x1 2.28 us: shards(): other = lax.ppermute(own, 'c', SWAP)]
    all_to_all x2 -> x3, blocking collectives: 42.9 us -> 45.6 us  [share(): lax.all_to_all(jnp.broadcast_to(array[None], (devices, *array.shape)), ax...]
  transfers between devices with their start and end apart: 0 -> 2, of which waited for: 0 -> 2; matrix products, arithmetic and copies ran while one was open for 0% -> 0% of each run, Pallas kernels for 0% -> 0%
where the time goes in v1:
time: 67.3 us; the launch traced here: 67 us
  blocking collectives  45.6 us (68%)
  Pallas kernels  14.3 us (21%)
  waiting for transfers between devices  3.31 us (5%)
  local copies, waits for them, and re-layouts  1.55 us (2%)
  other arithmetic  1.54 us (2%)
    all_to_all x3, blocking collectives, share(): lax.all_to_all(jnp.broadcast_to(array[None], (devices, *array.shape)), ax...  45.6 us
    pallas_call x1, Pallas kernels, ladder(): pl.pallas_call(ladder_kernel, out_shape=(jax.ShapeDtypeStruct(amps.shape,...  14.3 us
    ppermute x1, waiting for transfers between devices, shards(): other = lax.ppermute(own, 'c', SWAP)  2.28 us
    gather x1, local copies, waits for them, and re-layouts, shards(): owned = amplitudes[row_offset, col_offset]  1.37 us
  transfers between devices with their start and end apart: 2, of which 2 were waited for; matrix products, arithmetic and copies ran while one was open for 0% of the time, Pallas kernels for 0%

profile of v1, /device:TPU:0, one launch (start us, length us, event | category | flops | bytes accessed | tf_op | source)
XLA Modules:
  0.0 67.0 jit_solution(8655785007173117371)
XLA Ops:
  0.6 0.8 %fusion.3 = s32[8]{0:T(128)S(1)} fusion(s32[1024]{0:T(1024)} %param.5, s32[]{:T(128)S(6)} %select_n.21, s32[]{:T(128)S(6)} %mul.33, s32[]{:T(128)S(6)} %mul.32), kind=kLoop, calls=%fused_computation.10 | loop fusion | flops 200 | bytes 76 | tf_op jit(solution)/shard_map/concatenate | solution.py:112
  1.4 1.4 %gather_fusion = bf16[8,768]{1,0:T(8,128)(2,1)S(1)} fusion(bf16[100,50,768]{2,0,1:T(8,128)(2,1)} %param.3, s32[8]{0:T(128)S(1)} %fusion.3), kind=kCustom, calls=%fused_computation | custom fusion | bytes 24640 | tf_op jit(solution)/shard_map/gather | solution.py:112
  2.8 9.9 %all_to_all.15 = bf16[4,8,768]{2,1,0:T(8,128)(2,1)S(1)} all-to-all(bf16[4,8,768]{2,1,0:T(8,128)(2,1)S(1)} %broadcast_in_dim.29), channel_id=1, replica_groups=mesh['x'=4,'zh'=2,'zl'=2,'y'=4,'c'=2] {'y'}, dimensions={0} | all-to-all | bytes 98304 | tf_op jit(solution)/shard_map/all_to_all | solution.py:21
  12.7 0.1 broadcast_in_dim.31
  12.8 20.4 %all_to_all.16 = bf16[16,32,768]{2,1,0:T(8,128)(2,1)S(1)} all-to-all(bf16[16,32,768]{2,1,0:T(8,128)(2,1)S(1)} %broadcast_in_dim.31), channel_id=1, replica_groups=mesh['x'=4,'zh'=2,'zl'=2,'y'=4,'c'=2] {'x','zh','zl'}, dimensions={0} | all-to-all | bytes 1572864 | tf_op jit(solution)/shard_map/all_to_all | solution.py:21
  33.1 0.0 collective-permute-start
  33.1 2.3 %collective-permute-done.other_ref = bf16[64,8,768]{2,1,0:T(8,128)(2,1)S(1)} collective-permute-done((bf16[64,8,768]{2,1,0:T(8,128)(2,1)S(1)}, bf16[64,8,768]{2,1,0:T(8,128)(2,1)S(1)}, u32[]{:S(2)}, u32[]{:S(2)}) %collective-permute-start) | collective-permute-done | bytes 786464 | tf_op jit(solution)/shard_map/ppermute | solution.py:115
  35.4 14.3 %shard_map.50 = (bf16[50,100,768]{2,1,0:T(8,128)(2,1)}, f32[1,768]{1,0:T(1,128)S(1)}) custom-call(s32[1]{0:T(128)} %bitcast.core_ref, bf16[64,8,768]{2,1,0:T(8,128)(2,1)S(1)} %bitcast.7, bf16[64,8,768]{2,1,0:T(8,128)(2,1)S(1)} %collective-permute-done.other_ref, bf16[50,100,1024]{2,1,0:T(8,128)(2,1)} %bitcast.10, bf16[50,100,768]{2,1,0:T(8,128)(2,1)} %bitcast.9), custom_call_target="tpu_custom_call" | custom-call | flops 7864320000 | bytes 25600000 | tf_op jit(solution)/shard_map/pallas_call | solution.py:67
  49.7 0.1 collective-permute-start.1
  49.8 1.0 %collective-permute-done.1 = f32[1,768]{1,0:T(1,128)S(1)} collective-permute-done((f32[1,768]{1,0:T(1,128)S(1)}, f32[1,768]{1,0:T(1,128)S(1)}, u32[]{:S(2)}, u32[]{:S(2)}) %collective-permute-start.1) | collective-permute-done | bytes 3104 | tf_op jit(solution)/shard_map/ppermute | solution.py:120
  50.9 0.1 broadcast_in_dim.33
  51.0 15.3 %all_to_all.17 = f32[64,1,768]{2,1,0:T(1,128)S(1)} all-to-all(f32[64,1,768]{2,1,0:T(1,128)S(1)} %broadcast_in_dim.33), channel_id=1, replica_groups=mesh['x'=4,'zh'=2,'zl'=2,'y'=4,'c'=2] {'x','zh','zl','y'}, dimensions={0} | all-to-all | bytes 393216 | tf_op jit(solution)/shard_map/all_to_all | solution.py:21
  66.3 0.1 reduce_sum.9
  66.4 0.6 broadcast_multiply_fusion
  (2 shorter events, 0.0 us)
Async XLA Ops:
  33.1 2.3 %collective-permute-start = (bf16[64,8,768]{2,1,0:T(8,128)(2,1)S(1)}, bf16[64,8,768]{2,1,0:T(8,128)(2,1)S(1)}, u32[]{:S(2)}, u32[]{:S(2)}) collective-permute-start(bf16[64,8,768]{2,1,0:T(8,128)(2,1)S(1)} %bitcast.6), channel_id=1, source_target_pairs={{0,1},{1,0},{2,3},{3,2},{4,5},{5,4},{6,7},{7,6},{8,9},{9,8},{10,11... | collective-permute-start | bytes 2359304 | tf_op jit(solution)/shard_map/ppermute | solution.py:115
  49.7 1.2 %collective-permute-start.1 = (f32[1,768]{1,0:T(1,128)S(1)}, f32[1,768]{1,0:T(1,128)S(1)}, u32[]{:S(2)}, u32[]{:S(2)}) collective-permute-start(f32[1,768]{1,0:T(1,128)S(1)} %get-tuple-element.5), channel_id=1, source_target_pairs={{0,1},{1,0},{2,3},{3,2},{4,5},{5,4},{6,7},{7,6},{8,9},{9,8},{10,11... | collective-permute-start | bytes 9224 | tf_op jit(solution)/shard_map/ppermute | solution.py:120

commit v2 on v0

v2 whole, which is shorter than its diff:
```python
import functools

import jax
import jax.numpy as jnp
from jax import lax
from jax.experimental import pallas as pl
from jax.experimental.pallas import tpu as pltpu
from jax.sharding import Mesh
from jax.sharding import PartitionSpec as P

AXES = ("x", "zh", "zl", "y", "c")
ROW = ("x", "zh")
COL = ("zl", "y", "c")
CHIPS = ("x", "zh", "zl", "y")
PLANE = ("zh", "zl", "y")
SWAP = [(0, 1), (1, 0)]
RING = 4
ACROSS = [(x, (x + 2) % RING) for x in range(RING)]
BOTH_WAYS = [(2 * x, 2 * ((x + 1) % RING)) for x in range(RING)] + [
    (2 * x + 1, 2 * ((x - 1) % RING) + 1) for x in range(RING)
]
STEP_COLS = 10
LAST_COLS = 10
FIRST_VMEM = 16 << 20
LAST_VMEM = 24 << 20


def share(array, axes):
    devices = lax.axis_size(axes)
    return lax.all_to_all(
        jnp.broadcast_to(array[None], (devices, *array.shape)), axes, 0, 0, tiled=True
    )


def padded_rows(ref, nb):
    pad = -ref.shape[1] % 8

    def padded(block):
        if pad == 0:
            return block
        return jnp.concatenate([block, jnp.zeros((pad, block.shape[1]), block.dtype)], 0)

    return jnp.concatenate([padded(ref[j]) for j in range(nb)], 0)


def first_kernel(place_ref, mine_ref, theirs_ref, ints_ref, sum_ref, cols_ref):
    chunk, core = place_ref[0], place_ref[1]
    cols_ref[:, core] = mine_ref[...]
    cols_ref[:, 1 - core] = theirs_ref[...]
    blocks, rows, _ = ints_ref.shape
    depth, pairs = cols_ref.shape[0] * 2 * cols_ref.shape[2], cols_ref.shape[3]
    nb = STEP_COLS

    def body(block_ref):
        at = pl.ds(pl.program_id(0) * nb, nb)
        cols = cols_ref[...].reshape(depth, pairs)
        term = jnp.dot(padded_rows(block_ref, nb), cols, preferred_element_type=jnp.float32)
        sum_ref[at] = term.reshape(nb, -1, pairs)

    pltpu.emit_pipeline(
        body,
        grid=(blocks // nb,),
        in_specs=[pl.BlockSpec((nb, rows, depth), lambda s: (s, 0, chunk))],
        out_specs=[],
    )(ints_ref)


def last_kernel(
    place_ref, near_ref, far_ref, o_mine_ref, o_theirs_ref, ints_ref, sum_ref, amps_ref, res_ref, energy_ref, cols_ref, part_ref
):
    chunk, core = place_ref[0], place_ref[1]
    near = lax.rem(chunk + jnp.where(core == 0, RING - 1, 1), RING)
    far = lax.rem(chunk + jnp.where(core == 0, 1, RING - 1), RING)
    across = lax.rem(chunk + 2, RING)
    cols_ref[0, :, core] = near_ref[0]
    cols_ref[0, :, 1 - core] = near_ref[1]
    cols_ref[1, :, 1 - core] = far_ref[0]
    cols_ref[1, :, core] = far_ref[1]
    cols_ref[2, :, core] = o_mine_ref[...]
    cols_ref[2, :, 1 - core] = o_theirs_ref[...]
    part_ref[...] = jnp.zeros_like(part_ref)
    blocks, rows, _ = ints_ref.shape
    depth, pairs = cols_ref.shape[1] * 2 * cols_ref.shape[3], cols_ref.shape[4]
    nb = LAST_COLS
    whole = rows // 8 * 8

    def body(near_ints, far_ints, across_ints, out_ref):
        lhs = jnp.concatenate([padded_rows(r, nb) for r in (near_ints, far_ints, across_ints)], 1)
        cols = cols_ref[...].reshape(3 * depth, pairs)
        term = jnp.dot(lhs, cols, preferred_element_type=jnp.float32).reshape(nb, -1, pairs)
        for j in range(nb):
            at = pl.program_id(0) * nb + j
            full = (sum_ref[at] + term[j])[:rows]
            out_ref[j] = full.astype(jnp.bfloat16)
            product = amps_ref[at].astype(jnp.float32) * full
            part_ref[...] += jnp.sum(product[:whole].reshape(whole // 8, 8, -1), 0)
            if rows > whole:
                part_ref[: rows - whole] += product[whole:]

    pltpu.emit_pipeline(
        body,
        grid=(blocks // nb,),
        in_specs=[
            pl.BlockSpec((nb, rows, depth), lambda s: (s, 0, near)),
            pl.BlockSpec((nb, rows, depth), lambda s: (s, 0, far)),
            pl.BlockSpec((nb, rows, depth), lambda s: (s, 0, across)),
        ],
        out_specs=[pl.BlockSpec((nb, rows, pairs), lambda s: (s, 0, 0))],
    )(ints_ref, ints_ref, ints_ref, res_ref)
    energy_ref[...] = jnp.sum(part_ref[...], 0, keepdims=True)


VMEM_SPEC = pl.BlockSpec(memory_space=pltpu.VMEM)
HBM_SPEC = pl.BlockSpec(memory_space=pltpu.HBM)
SMEM_SPEC = pl.BlockSpec(memory_space=pltpu.SMEM)


def first_chunk(place, mine, theirs, ints):
    blocks, rows, window = ints.shape
    pairs = mine.shape[2]
    depth = window // RING
    return pl.pallas_call(
        first_kernel,
        out_shape=pltpu.VMEM((blocks, rows + -rows % 8, pairs), jnp.float32),
        in_specs=[SMEM_SPEC, VMEM_SPEC, VMEM_SPEC, HBM_SPEC],
        out_specs=VMEM_SPEC,
        scratch_shapes=[pltpu.VMEM((mine.shape[0], 2, *mine.shape[1:]), mine.dtype)],
        compiler_params=pltpu.CompilerParams(vmem_limit_bytes=FIRST_VMEM),
        cost_estimate=pl.CostEstimate(
            flops=2 * blocks * rows * depth * pairs, bytes_accessed=2 * blocks * rows * depth, transcendentals=0
        ),
    )(place, mine, theirs, ints)


def last_chunks(place, near, far, o_mine, o_theirs, ints, total, amps):
    blocks, rows, window = ints.shape
    pairs = amps.shape[2]
    depth = window // RING
    return pl.pallas_call(
        last_kernel,
        out_shape=(
            jax.ShapeDtypeStruct(amps.shape, jnp.bfloat16),
            jax.ShapeDtypeStruct((1, pairs), jnp.float32),
        ),
        in_specs=[SMEM_SPEC, VMEM_SPEC, VMEM_SPEC, VMEM_SPEC, VMEM_SPEC, HBM_SPEC, VMEM_SPEC, VMEM_SPEC],
        out_specs=(HBM_SPEC, VMEM_SPEC),
        scratch_shapes=[
            pltpu.VMEM((RING - 1, o_mine.shape[0], 2, *o_mine.shape[1:]), o_mine.dtype),
            pltpu.VMEM((8, pairs), jnp.float32),
        ],
        compiler_params=pltpu.CompilerParams(vmem_limit_bytes=LAST_VMEM),
        cost_estimate=pl.CostEstimate(
            flops=6 * blocks * rows * depth * pairs,
            bytes_accessed=2 * blocks * rows * (3 * depth + 2 * pairs),
            transcendentals=0,
        ),
    )(place, near, far, o_mine, o_theirs, ints, total, amps)


def shards(amplitudes, integrals, window_index):
    block_rows, block_cols, pairs = amplitudes.shape
    window = integrals.shape[2]
    per_device = window // lax.axis_size(AXES)
    row_rank = lax.axis_index(ROW)
    col_rank = lax.axis_index(COL)
    virtuals = block_rows * lax.axis_size(ROW)
    owned_index = lax.dynamic_slice_in_dim(window_index, lax.axis_index(AXES) * per_device, per_device)
    row_offset = owned_index // virtuals - row_rank * block_rows
    col_offset = owned_index % virtuals - col_rank * block_cols
    owned = amplitudes[row_offset, col_offset]
    ints, amps = integrals.transpose(1, 0, 2), amplitudes.transpose(1, 0, 2)

    ints = pltpu.with_memory_space_constraint(ints, pltpu.HBM)
    place = jnp.stack([lax.axis_index("x"), lax.axis_index("c")])

    mine = share(owned, PLANE)
    theirs = lax.ppermute(mine, "c", SWAP)
    o_mine = lax.ppermute(mine, "x", ACROSS)
    near = lax.ppermute(jnp.stack([mine, theirs]), ("x", "c"), BOTH_WAYS)
    total = first_chunk(place, mine, theirs, ints)
    near, o_mine, total = lax.optimization_barrier((near, o_mine, total))
    o_theirs = lax.ppermute(o_mine, "c", SWAP)
    far = lax.ppermute(near, "c", SWAP)
    residual, energy = last_chunks(place, near, far, o_mine, o_theirs, ints, total, amps)

    chip = energy + lax.ppermute(energy, "c", SWAP)
    total_energy = jnp.sum(share(chip, CHIPS), axis=(0, 1))
    return residual.transpose(1, 0, 2), total_energy / virtuals


def solution(mesh):
    finer = Mesh(mesh.devices.reshape(4, 2, 2, 4, 2), AXES)
    placed = (P(ROW, COL, None), P(ROW, COL, None), P())
    return jax.shard_map(
        shards, mesh=finer, in_specs=placed, out_specs=(P(ROW, COL, None), P()), check_vma=False
    )
```

time: 103 us -> 65.4 us (0.63); the launches traced: 101 us -> 65 us
  blocking collectives: 74.5 us -> 30.6 us
  Pallas kernels: 0 us -> 17.4 us
  matrix products: 16.5 us -> 0 us
  waiting for transfers between devices: 0 us -> 8.12 us
  other arithmetic: 8.16 us -> 1.66 us
  starting transfers between devices: 0 us -> 5.01 us
    psum x5 -> x0, blocking collectives: 31.6 us -> none  [one_axis_at_a_time(): return functools.reduce(lax.psum, axes, array)]
    pallas_call x0 -> x2, Pallas kernels: none -> 17.4 us  [the longest x1 11.6 us: last_chunks(): pl.pallas_call(last_kernel, out_shape=(jax.ShapeDtypeStruct(amps.shape, j...]
    dot_general x1 -> x0, matrix products: 16.5 us -> none  [shards(): jnp.einsum('abk,kp->abp', integrals, columns, preferred_element_type=jnp....]
    all_to_all x2, blocking collectives: 42.9 us -> 30.6 us  [share(): lax.all_to_all(jnp.broadcast_to(array[None], (devices, *array.shape)), ax...]
    ppermute x0 -> x6, waiting for transfers between devices: none -> 8.12 us  [the longest x1 4.15 us: shards(): o_mine = lax.ppermute(mine, 'x', ACROSS)]
    reduce_sum x1, other arithmetic: 6.78 us -> 0.15 us  [shards(): total_energy = jnp.sum(share(chip, CHIPS), axis=(0, 1))]
    ppermute x0 -> x6, starting transfers between devices: none -> 5.01 us  [the longest x1 2.73 us: shards(): o_mine = lax.ppermute(mine, 'x', ACROSS)]
  transfers between devices with their start and end apart: 0 -> 6, of which waited for: 0 -> 4; matrix products, arithmetic and copies ran while one was open for 0% -> 0% of each run, Pallas kernels for 0% -> 9%
where the time goes in v2:
time: 65.4 us; the launch traced here: 65 us
  blocking collectives  30.6 us (47%)
  Pallas kernels  17.4 us (27%)
  waiting for transfers between devices  8.12 us (12%)
  starting transfers between devices  5.01 us (8%)
  other arithmetic  1.66 us (3%)
  local copies, waits for them, and re-layouts  1.5 us (2%)
  between operations  0.69 us (1%)
    all_to_all x2, blocking collectives, share(): lax.all_to_all(jnp.broadcast_to(array[None], (devices, *array.shape)), ax...  30.6 us
    pallas_call x1, Pallas kernels, last_chunks(): pl.pallas_call(last_kernel, out_shape=(jax.ShapeDtypeStruct(amps.shape, j...  11.6 us
    pallas_call x1, Pallas kernels, first_chunk(): pl.pallas_call(first_kernel, out_shape=pltpu.VMEM((blocks, rows + -rows %...  5.74 us
    ppermute x1, waiting for transfers between devices, shards(): o_mine = lax.ppermute(mine, 'x', ACROSS)  4.15 us
    ppermute x1, starting transfers between devices, shards(): o_mine = lax.ppermute(mine, 'x', ACROSS)  2.73 us
    ppermute x1, starting transfers between devices, shards(): near = lax.ppermute(jnp.stack([mine, theirs]), ('x', 'c'), BOTH_WAYS)  1.56 us
    ppermute x1, waiting for transfers between devices, shards(): o_theirs = lax.ppermute(o_mine, 'c', SWAP)  1.49 us
    ppermute x1, waiting for transfers between devices, shards(): theirs = lax.ppermute(mine, 'c', SWAP)  1.44 us
  transfers between devices with their start and end apart: 6, of which 4 were waited for; matrix products, arithmetic and copies ran while one was open for 0% of the time, Pallas kernels for 9%

profile of v2, /device:TPU:0, one launch (start us, length us, event | category | flops | bytes accessed | tf_op | source)
XLA Modules:
  0.0 65.0 jit_solution(12270053526252673279)
XLA Ops:
  0.6 0.8 %fusion.3 = s32[8]{0:T(128)S(1)} fusion(s32[1024]{0:T(1024)} %param.5, s32[]{:T(128)S(6)} %select_n.21, s32[]{:T(128)S(6)} %mul.33, s32[]{:T(128)S(6)} %mul.32), kind=kLoop, calls=%fused_computation.11 | loop fusion | flops 200 | bytes 76 | tf_op jit(solution)/shard_map/concatenate | solution.py:170
  1.4 1.4 %gather_fusion = bf16[8,768]{1,0:T(8,128)(2,1)S(1)} fusion(bf16[100,50,768]{2,0,1:T(8,128)(2,1)} %param.3, s32[8]{0:T(128)S(1)} %fusion.3), kind=kCustom, calls=%fused_computation | custom fusion | bytes 24640 | tf_op jit(solution)/shard_map/gather | solution.py:170
  2.8 16.3 %all_to_all.10.mine_ref = bf16[16,8,768]{2,1,0:T(8,128)(2,1)S(1)} all-to-all(bf16[16,8,768]{2,1,0:T(8,128)(2,1)S(1)} %broadcast_in_dim.22), channel_id=1, replica_groups=mesh['x'=4,'zh'=2,'zl'=2,'y'=4,'c'=2] {'zh','zl','y'}, dimensions={0} | all-to-all | bytes 393216 | tf_op jit(solution)/shard_map/all_to_all | solution.py:30
  19.1 0.0 collective-permute-start
  19.1 1.4 %collective-permute-done.theirs_ref = bf16[16,8,768]{2,1,0:T(8,128)(2,1)S(1)} collective-permute-done((bf16[16,8,768]{2,1,0:T(8,128)(2,1)S(1)}, bf16[16,8,768]{2,1,0:T(8,128)(2,1)S(1)}, u32[]{:S(2)}, u32[]{:S(2)}) %collective-permute-start) | collective-permute-done | bytes 196640 | tf_op jit(solution)/shard_map/ppermute | solution.py:177
  20.5 0.0 slice-start
  20.6 1.6 %collective-permute-start.1 = (bf16[2,16,8,768]{3,2,1,0:T(8,128)(2,1)S(1)}, bf16[2,16,8,768]{3,2,1,0:T(8,128)(2,1)S(1)}, u32[]{:S(2)}, u32[]{:S(2)}) collective-permute-start(bf16[2,16,8,768]{3,2,1,0:T(8,128)(2,1)S(1)} %pad_maximum_fusion), channel_id=1, source_target_pairs={{0,32},{32,64},{64,96},{96,0},{1,97},{33,1},{65,33},{97,65},{2,34}... | collective-permute-start | bytes 1179656 | tf_op jit(solution)/shard_map/ppermute | solution.py:179
  22.1 2.7 %collective-permute-start.2 = (bf16[16,8,768]{2,1,0:T(8,128)(2,1)S(1)}, bf16[16,8,768]{2,1,0:T(8,128)(2,1)S(1)}, u32[]{:S(2)}, u32[]{:S(2)}) collective-permute-start(bf16[16,8,768]{2,1,0:T(8,128)(2,1)S(1)} %all_to_all.10.mine_ref), channel_id=1, source_target_pairs={{0,64},{32,96},{64,0},{96,32},{1,65},{33,97},{65,1},{97,33},{2,66}... | collective-permute-start | bytes 589832 | tf_op jit(solution)/shard_map/ppermute | solution.py:178
  24.9 0.1 pad_add_fusion.place_ref
  24.9 0.0 slice-start.1
  24.9 5.7 %shard_map.50.sum_ref = f32[50,104,768]{2,1,0:T(8,128)S(1)} custom-call(s32[2]{0:T(128)S(1)} %pad_add_fusion.place_ref, bf16[16,8,768]{2,1,0:T(8,128)(2,1)S(1)} %all_to_all.10.mine_ref, bf16[16,8,768]{2,1,0:T(8,128)(2,1)S(1)} %collective-permute-done.theirs_ref, bf16[50,100,1024]{2,1,0:T(8,128)(2,1)} %bitcast.12), custom_call_target="tpu_custom_call" | custom-call | flops 1966080000 | bytes 2560000 | tf_op jit(solution)/shard_map/pallas_call | solution.py:122
  30.7 4.1 %collective-permute-done.2.o_mine_ref = bf16[16,8,768]{2,1,0:T(8,128)(2,1)S(1)} collective-permute-done((bf16[16,8,768]{2,1,0:T(8,128)(2,1)S(1)}, bf16[16,8,768]{2,1,0:T(8,128)(2,1)S(1)}, u32[]{:S(2)}, u32[]{:S(2)}) %collective-permute-start.2) | collective-permute-done | bytes 196640 | tf_op jit(solution)/shard_map/ppermute | solution.py:178
  34.8 0.0 collective-permute-done.1.near_ref
  34.8 0.0 collective-permute-start.3
  34.8 0.5 collective-permute-start.4
  35.4 1.5 %collective-permute-done.4.o_theirs_ref = bf16[16,8,768]{2,1,0:T(8,128)(2,1)S(1)} collective-permute-done((bf16[16,8,768]{2,1,0:T(8,128)(2,1)S(1)}, bf16[16,8,768]{2,1,0:T(8,128)(2,1)S(1)}, u32[]{:S(2)}, u32[]{:S(2)}) %collective-permute-start.4) | collective-permute-done | bytes 196640 | tf_op jit(solution)/shard_map/ppermute | solution.py:182
  36.8 0.0 collective-permute-done.3.far_ref
  36.8 0.0 slice-done
  36.9 0.0 slice-done.1
  36.9 11.6 %shard_map.51 = (bf16[50,100,768]{2,1,0:T(8,128)(2,1)}, f32[1,768]{1,0:T(1,128)S(1)}) custom-call(s32[2]{0:T(128)S(1)} %pad_add_fusion.place_ref, bf16[2,16,8,768]{3,2,1,0:T(8,128)(2,1)S(1)} %collective-permute-done.1.near_ref, bf16[2,16,8,768]{3,2,1,0:T(8,128)(2,1)S(1)} %collective-permute-done.3.far_ref, ...), custom_call_target="tpu_custom_call" | custom-call | flops 5898240000 | bytes 23040000 | tf_op jit(solution)/shard_map/pallas_call | solution.py:139
  48.5 0.2 collective-permute-start.5
  48.7 1.0 %collective-permute-done.5 = f32[1,768]{1,0:T(1,128)S(1)} collective-permute-done((f32[1,768]{1,0:T(1,128)S(1)}, f32[1,768]{1,0:T(1,128)S(1)}, u32[]{:S(2)}, u32[]{:S(2)}) %collective-permute-start.5) | collective-permute-done | bytes 3104 | tf_op jit(solution)/shard_map/ppermute | solution.py:186
  49.8 0.1 broadcast_in_dim.24
  49.9 14.4 %all_to_all.11 = f32[64,1,768]{2,1,0:T(1,128)S(1)} all-to-all(f32[64,1,768]{2,1,0:T(1,128)S(1)} %broadcast_in_dim.24), channel_id=1, replica_groups=mesh['x'=4,'zh'=2,'zl'=2,'y'=4,'c'=2] {'x','zh','zl','y'}, dimensions={0} | all-to-all | bytes 393216 | tf_op jit(solution)/shard_map/all_to_all | solution.py:30
  64.2 0.1 reduce_sum.9
  64.4 0.6 broadcast_multiply_fusion
  (4 shorter events, 0.1 us)
Async XLA Ops:
  19.1 1.4 %collective-permute-start = (bf16[16,8,768]{2,1,0:T(8,128)(2,1)S(1)}, bf16[16,8,768]{2,1,0:T(8,128)(2,1)S(1)}, u32[]{:S(2)}, u32[]{:S(2)}) collective-permute-start(bf16[16,8,768]{2,1,0:T(8,128)(2,1)S(1)} %all_to_all.10.mine_ref), channel_id=1, source_target_pairs={{0,1},{1,0},{2,3},{3,2},{4,5},{5,4},{6,7},{7,6},{8,9},{9,8},{10,11... | collective-permute-start | bytes 589832 | tf_op jit(solution)/shard_map/ppermute | solution.py:177
  20.5 16.3 %slice-start = ((s8[7987200]{0:T(1024)(128)(4,1)}), s8[4194304]{0:T(1024)(128)(4,1)S(1)}, s32[]{:S(2)}) async-start(s8[7987200]{0:T(1024)(128)(4,1)} %bitcast.7), calls=%async_computation.2 | async-start | bytes 8388608
  20.6 14.3 %collective-permute-start.1 = (bf16[2,16,8,768]{3,2,1,0:T(8,128)(2,1)S(1)}, bf16[2,16,8,768]{3,2,1,0:T(8,128)(2,1)S(1)}, u32[]{:S(2)}, u32[]{:S(2)}) collective-permute-start(bf16[2,16,8,768]{3,2,1,0:T(8,128)(2,1)S(1)} %pad_maximum_fusion), channel_id=1, source_target_pairs={{0,32},{32,64},{64,96},{96,0},{1,97},{33,1},{65,33},{97,65},{2,34}... | collective-permute-start | bytes 1179656 | tf_op jit(solution)/shard_map/ppermute | solution.py:179
  22.1 12.7 %collective-permute-start.2 = (bf16[16,8,768]{2,1,0:T(8,128)(2,1)S(1)}, bf16[16,8,768]{2,1,0:T(8,128)(2,1)S(1)}, u32[]{:S(2)}, u32[]{:S(2)}) collective-permute-start(bf16[16,8,768]{2,1,0:T(8,128)(2,1)S(1)} %all_to_all.10.mine_ref), channel_id=1, source_target_pairs={{0,64},{32,96},{64,0},{96,32},{1,65},{33,97},{65,1},{97,33},{2,66}... | collective-permute-start | bytes 589832 | tf_op jit(solution)/shard_map/ppermute | solution.py:178
  24.9 11.9 %slice-start.1 = ((s8[7987200]{0:T(1024)(128)(4,1)}), s8[3792896]{0:T(1024)(128)(4,1)S(1)}, s32[]{:S(2)}) async-start(s8[7987200]{0:T(1024)(128)(4,1)} %bitcast.7), calls=%async_computation.3 | async-start | bytes 7585792
  34.8 2.0 %collective-permute-start.3 = (bf16[2,16,8,768]{3,2,1,0:T(8,128)(2,1)S(1)}, bf16[2,16,8,768]{3,2,1,0:T(8,128)(2,1)S(1)}, u32[]{:S(2)}, u32[]{:S(2)}) collective-permute-start(bf16[2,16,8,768]{3,2,1,0:T(8,128)(2,1)S(1)} %collective-permute-done.1.near_ref), channel_id=1, source_target_pairs={{0,1},{1,0},{2,3},{3,2},{4,5},{5,4},{6,7},{7,6},{8,9},{9,8},{10,11... | collective-permute-start | bytes 1179656 | tf_op jit(solution)/shard_map/ppermute | solution.py:183
  34.8 2.0 %collective-permute-start.4 = (bf16[16,8,768]{2,1,0:T(8,128)(2,1)S(1)}, bf16[16,8,768]{2,1,0:T(8,128)(2,1)S(1)}, u32[]{:S(2)}, u32[]{:S(2)}) collective-permute-start(bf16[16,8,768]{2,1,0:T(8,128)(2,1)S(1)} %collective-permute-done.2.o_mine_ref), channel_id=1, source_target_pairs={{0,1},{1,0},{2,3},{3,2},{4,5},{5,4},{6,7},{7,6},{8,9},{9,8},{10,11... | collective-permute-start | bytes 589832 | tf_op jit(solution)/shard_map/ppermute | solution.py:182
  48.5 1.2 %collective-permute-start.5 = (f32[1,768]{1,0:T(1,128)S(1)}, f32[1,768]{1,0:T(1,128)S(1)}, u32[]{:S(2)}, u32[]{:S(2)}) collective-permute-start(f32[1,768]{1,0:T(1,128)S(1)} %get-tuple-element.11), channel_id=1, source_target_pairs={{0,1},{1,0},{2,3},{3,2},{4,5},{5,4},{6,7},{7,6},{8,9},{9,8},{10,11... | collective-permute-start | bytes 9224 | tf_op jit(solution)/shard_map/ppermute | solution.py:186

commit v3 on v0

v3 whole, which is shorter than its diff:
```python
import functools

import jax
import jax.numpy as jnp
from jax import lax
from jax.experimental import pallas as pl
from jax.experimental.pallas import tpu as pltpu
from jax.sharding import Mesh
from jax.sharding import PartitionSpec as P

AXES = ("x", "zh", "zl", "y", "c")
ROW = ("x", "zh")
COL = ("zl", "y", "c")
CHIPS = ("x", "zh", "zl", "y")
SWAP = [(0, 1), (1, 0)]
RING = 4


def device(x, z, y, core):
    return ((x * RING + z) * RING + y) * 2 + core


def plane_groups():
    ring = range(RING)
    of_x = [[device(x, z, y, 0) for z in ring for y in ring] for x in ring]
    of_z = [[device(x, z, y, 1) for x in ring for y in ring] for z in ring]
    return of_x + of_z


def turned(by):
    ring = range(RING)
    return [
        (device(x, z, y, 0), device((x + by) % RING, z, y, 0)) for x in ring for z in ring for y in ring
    ] + [(device(x, z, y, 1), device(x, (z + by) % RING, y, 1)) for x in ring for z in ring for y in ring]


LAST_COLS = 10
LANES = 256
FETCH_VMEM = 4 << 20
LAST_VMEM = 16 << 20


def share(array, axes, groups=None):
    devices = lax.axis_size(axes) if groups is None else len(groups[0])
    return lax.all_to_all(
        jnp.broadcast_to(array[None], (devices, *array.shape)),
        axes,
        0,
        0,
        axis_index_groups=groups,
        tiled=True,
    )


def padded_rows(ref, nb):
    pad = -ref.shape[1] % 8

    def padded(block):
        if pad == 0:
            return block
        return jnp.concatenate([block, jnp.zeros((pad, block.shape[1]), block.dtype)], 0)

    return jnp.concatenate([padded(ref[j]) for j in range(nb)], 0)


VMEM_SPEC = pl.BlockSpec(memory_space=pltpu.VMEM)
HBM_SPEC = pl.BlockSpec(memory_space=pltpu.HBM)
SMEM_SPEC = pl.BlockSpec(memory_space=pltpu.SMEM)


def fetch_kernel(after_ref, ints_ref, amps_ref, ints_out, amps_out, token_out, sems):
    token_out[...] = after_ref[0]
    copies = [
        pltpu.make_async_copy(ints_ref, ints_out, sems.at[0]),
        pltpu.make_async_copy(amps_ref, amps_out, sems.at[1]),
    ]
    for copy in copies:
        copy.start()
    for copy in copies:
        copy.wait()


def fetch(after, ints, amps):
    return pl.pallas_call(
        fetch_kernel,
        out_shape=tuple(pltpu.VMEM(a.shape, a.dtype) for a in (ints, amps, after[0])),
        in_specs=[VMEM_SPEC, HBM_SPEC, HBM_SPEC],
        out_specs=(VMEM_SPEC, VMEM_SPEC, VMEM_SPEC),
        scratch_shapes=[pltpu.SemaphoreType.DMA((2,))],
        compiler_params=pltpu.CompilerParams(vmem_limit_bytes=FETCH_VMEM),
        cost_estimate=pl.CostEstimate(
            flops=0, bytes_accessed=2 * (ints.size + amps.size), transcendentals=0
        ),
    )(after, *(pltpu.with_memory_space_constraint(a, pltpu.HBM) for a in (ints, amps)))


def ladder_kernel(place_ref, *refs):
    mine, theirs = refs[:RING], refs[RING : 2 * RING]
    ints_ref, amps_ref, _, res_ref, energy_ref, cols_ref, part_ref = refs[2 * RING :]
    x, z, core = place_ref[0], place_ref[1], place_ref[2]
    pairs = amps_ref.shape[2]

    def put(of_core_0, of_core_1):
        for turn in range(RING):
            plane = (RING, RING, *of_core_0[turn].shape[1:])
            cols_ref[lax.rem(x + turn, RING), :, :, 0] = of_core_0[turn][...].reshape(plane)
            cols_ref[:, lax.rem(z + turn, RING), :, 1] = of_core_1[turn][...].reshape(plane)

    @pl.when(core == 0)
    def _():
        put(mine, theirs)

    @pl.when(core != 0)
    def _():
        put(theirs, mine)

    part_ref[...] = jnp.zeros_like(part_ref)
    blocks, rows, window = ints_ref.shape
    nb = LAST_COLS
    whole = rows // 8 * 8

    def body(out_ref):
        start = pl.program_id(0) * nb
        lhs = padded_rows(ints_ref.at[pl.ds(start, nb)], nb)
        cols = cols_ref[...].reshape(window, pairs)
        for at in range(0, pairs, LANES):
            cut = slice(at, at + LANES)
            total = jnp.dot(lhs, cols[:, cut], preferred_element_type=jnp.float32)
            total = total.reshape(nb, -1, LANES)
            for j in range(nb):
                full = total[j, :rows]
                out_ref[j, :, cut] = full.astype(jnp.bfloat16)
                product = amps_ref[start + j, :, cut].astype(jnp.float32) * full
                part_ref[:, cut] += jnp.sum(product[:whole].reshape(whole // 8, 8, -1), 0)
                if rows > whole:
                    part_ref[: rows - whole, cut] += product[whole:]

    pltpu.emit_pipeline(
        body,
        grid=(blocks // nb,),
        in_specs=[],
        out_specs=[pl.BlockSpec((nb, rows, pairs), lambda s: (s, 0, 0))],
    )(res_ref)
    energy_ref[...] = jnp.sum(part_ref[...], 0, keepdims=True)


def ladder(place, mine, theirs, ints, amps, token):
    blocks, rows, window = ints.shape
    pairs = amps.shape[2]
    return pl.pallas_call(
        ladder_kernel,
        out_shape=(
            jax.ShapeDtypeStruct(amps.shape, jnp.bfloat16),
            jax.ShapeDtypeStruct((1, pairs), jnp.float32),
        ),
        in_specs=[SMEM_SPEC] + [VMEM_SPEC] * (2 * RING + 3),
        out_specs=(HBM_SPEC, VMEM_SPEC),
        scratch_shapes=[
            pltpu.VMEM((RING, RING, RING, 2, *mine[0].shape[1:]), mine[0].dtype),
            pltpu.VMEM((8, pairs), jnp.float32),
        ],
        compiler_params=pltpu.CompilerParams(vmem_limit_bytes=LAST_VMEM),
        cost_estimate=pl.CostEstimate(
            flops=2 * blocks * rows * window * pairs,
            bytes_accessed=2 * blocks * rows * (window + 2 * pairs),
            transcendentals=0,
        ),
    )(place, *mine, *theirs, ints, amps, token)


def shards(amplitudes, integrals, window_index):
    block_rows, block_cols, pairs = amplitudes.shape
    window = integrals.shape[2]
    per_device = window // lax.axis_size(AXES)
    row_rank = lax.axis_index(ROW)
    col_rank = lax.axis_index(COL)
    virtuals = block_rows * lax.axis_size(ROW)
    owned_index = lax.dynamic_slice_in_dim(window_index, lax.axis_index(AXES) * per_device, per_device)
    row_offset = owned_index // virtuals - row_rank * block_rows
    col_offset = owned_index % virtuals - col_rank * block_cols
    owned = amplitudes[row_offset, col_offset]
    ints, amps = integrals.transpose(1, 0, 2), amplitudes.transpose(1, 0, 2)
    place = jnp.stack([lax.axis_index("x"), lax.axis_index(("zh", "zl")), lax.axis_index("c")])

    owned, place = lax.optimization_barrier((owned, place))
    plane = share(owned, AXES, plane_groups())
    swapped = lambda array: lax.ppermute(array, "c", SWAP)
    across = lax.ppermute(plane, AXES, turned(2))
    above = lax.ppermute(plane, AXES, turned(-1))
    below = lax.ppermute(plane, AXES, turned(1))
    there = swapped(plane)
    ints, amps, token = fetch(there, ints, amps)
    above, across, below, token = lax.optimization_barrier((above, across, below, token))
    mine = (plane, above, across, below)
    theirs = (there, swapped(above), swapped(across), swapped(below))
    residual, energy = ladder(place, mine, theirs, ints, amps, token)

    chip = energy + lax.ppermute(energy, "c", SWAP)
    total_energy = jnp.sum(share(chip, CHIPS), axis=(0, 1))
    return residual.transpose(1, 0, 2), total_energy / virtuals


def solution(mesh):
    finer = Mesh(mesh.devices.reshape(4, 2, 2, 4, 2), AXES)
    placed = (P(ROW, COL, None), P(ROW, COL, None), P())
    return jax.shard_map(
        shards, mesh=finer, in_specs=placed, out_specs=(P(ROW, COL, None), P()), check_vma=False
    )
```

time: 103 us -> 62.2 us (0.60); the launches traced: 101 us -> 61.9 us
  blocking collectives: 74.5 us -> 32 us
  Pallas kernels: 0 us -> 17.6 us
  matrix products: 16.5 us -> 0 us
  other arithmetic: 8.16 us -> 1.62 us
  starting transfers between devices: 0 us -> 6.16 us
  waiting for transfers between devices: 0 us -> 2.35 us
    psum x5 -> x0, blocking collectives: 31.6 us -> none  [one_axis_at_a_time(): return functools.reduce(lax.psum, axes, array)]
    pallas_call x0 -> x2, Pallas kernels: none -> 17.6 us  [the longest x1 11.3 us: ladder(): pl.pallas_call(ladder_kernel, out_shape=(jax.ShapeDtypeStruct(amps.shape,...]
    dot_general x1 -> x0, matrix products: 16.5 us -> none  [shards(): jnp.einsum('abk,kp->abp', integrals, columns, preferred_element_type=jnp....]
    all_to_all x2, blocking collectives: 42.9 us -> 32 us  [share(): lax.all_to_all(jnp.broadcast_to(array[None], (devices, *array.shape)), ax...]
    reduce_sum x1, other arithmetic: 6.78 us -> 0.15 us  [shards(): total_energy = jnp.sum(share(chip, CHIPS), axis=(0, 1))]
    ppermute x0 -> x8, starting transfers between devices: none -> 6.16 us  [the longest x1 2.53 us: shards(): across = lax.ppermute(plane, AXES, turned(2))]
    ppermute x0 -> x8, waiting for transfers between devices: none -> 2.35 us  [the longest x4 1.4 us: shards(): swapped = lambda array: lax.ppermute(array, 'c', SWAP)]
  transfers between devices with their start and end apart: 0 -> 8, of which waited for: 0 -> 4; matrix products, arithmetic and copies ran while one was open for 0% -> 0% of each run, Pallas kernels for 0% -> 10%
where the time goes in v3:
time: 62.2 us; the launch traced here: 61.9 us
  blocking collectives  32 us (51%)
  Pallas kernels  17.6 us (28%)
  starting transfers between devices  6.16 us (10%)
  waiting for transfers between devices  2.35 us (4%)
  other arithmetic  1.62 us (3%)
  local copies, waits for them, and re-layouts  1.49 us (2%)
  between operations  0.71 us (1%)
    all_to_all x2, blocking collectives, share(): lax.all_to_all(jnp.broadcast_to(array[None], (devices, *array.shape)), ax...  32 us
    pallas_call x1, Pallas kernels, ladder(): pl.pallas_call(ladder_kernel, out_shape=(jax.ShapeDtypeStruct(amps.shape,...  11.3 us
    pallas_call x1, Pallas kernels, fetch(): pl.pallas_call(fetch_kernel, out_shape=tuple((pltpu.VMEM(a.shape, a.dtype...  6.31 us
    ppermute x1, starting transfers between devices, shards(): across = lax.ppermute(plane, AXES, turned(2))  2.53 us
    ppermute x4, waiting for transfers between devices, shards(): swapped = lambda array: lax.ppermute(array, 'c', SWAP)  1.4 us
    gather x1, local copies, waits for them, and re-layouts, shards(): owned = amplitudes[row_offset, col_offset]  1.37 us
    ppermute x1, starting transfers between devices, shards(): above = lax.ppermute(plane, AXES, turned(-1))  1.36 us
    ppermute x1, starting transfers between devices, shards(): below = lax.ppermute(plane, AXES, turned(1))  1.29 us
  transfers between devices with their start and end apart: 8, of which 4 were waited for; matrix products, arithmetic and copies ran while one was open for 0% of the time, Pallas kernels for 10%

profile of v3, /device:TPU:0, one launch (start us, length us, event | category | flops | bytes accessed | tf_op | source)
XLA Modules:
  0.0 61.9 jit_solution(13824676819950425026)
XLA Ops:
  0.6 0.8 %fusion.3 = s32[8]{0:T(128)S(1)} fusion(s32[1024]{0:T(1024)} %param.5, s32[]{:T(128)S(6)} %select_n.21, s32[]{:T(128)S(6)} %mul.36, s32[]{:T(128)S(6)} %mul.35), kind=kLoop, calls=%fused_computation.10 | loop fusion | flops 200 | bytes 76 | tf_op jit(solution)/shard_map/concatenate | solution.py:181
  1.4 1.4 %gather_fusion = bf16[8,768]{1,0:T(8,128)(2,1)S(1)} fusion(bf16[100,50,768]{2,0,1:T(8,128)(2,1)} %param.3, s32[8]{0:T(128)S(1)} %fusion.3), kind=kCustom, calls=%fused_computation | custom fusion | bytes 24640 | tf_op jit(solution)/shard_map/gather | solution.py:181
  2.8 0.1 pad_add_fusion.place_ref
  2.9 16.9 %all_to_all.10.refs_0_ = bf16[16,8,768]{2,1,0:T(8,128)(2,1)S(1)} all-to-all(bf16[16,8,768]{2,1,0:T(8,128)(2,1)S(1)} %broadcast_in_dim.22), channel_id=1, replica_groups={{0,2,4,6,8,10,12,14,16,18,20,22,24,26,28,30},{32,34,36,38,40,42,44,46,4..., dimensions={0} | all-to-all | bytes 393216 | tf_op jit(solution)/shard_map/all_to_all | solution.py:45
  19.8 0.0 collective-permute-start.3
  19.8 1.3 %collective-permute-start.2 = (bf16[16,8,768]{2,1,0:T(8,128)(2,1)S(1)}, bf16[16,8,768]{2,1,0:T(8,128)(2,1)S(1)}, u32[]{:S(2)}, u32[]{:S(2)}) collective-permute-start(bf16[16,8,768]{2,1,0:T(8,128)(2,1)S(1)} %all_to_all.10.refs_0_), channel_id=1, source_target_pairs={{0,32},{2,34},{4,36},{6,38},{8,40},{10,42},{12,44},{14,46},{16,48}... | collective-permute-start | bytes 589832 | tf_op jit(solution)/shard_map/ppermute | solution.py:190
  21.1 2.5 %collective-permute-start.1 = (bf16[16,8,768]{2,1,0:T(8,128)(2,1)S(1)}, bf16[16,8,768]{2,1,0:T(8,128)(2,1)S(1)}, u32[]{:S(2)}, u32[]{:S(2)}) collective-permute-start(bf16[16,8,768]{2,1,0:T(8,128)(2,1)S(1)} %all_to_all.10.refs_0_), channel_id=1, source_target_pairs={{0,64},{2,66},{4,68},{6,70},{8,72},{10,74},{12,76},{14,78},{16,80}... | collective-permute-start | bytes 589832 | tf_op jit(solution)/shard_map/ppermute | solution.py:188
  23.7 1.4 %collective-permute-start = (bf16[16,8,768]{2,1,0:T(8,128)(2,1)S(1)}, bf16[16,8,768]{2,1,0:T(8,128)(2,1)S(1)}, u32[]{:S(2)}, u32[]{:S(2)}) collective-permute-start(bf16[16,8,768]{2,1,0:T(8,128)(2,1)S(1)} %all_to_all.10.refs_0_), channel_id=1, source_target_pairs={{0,96},{2,98},{4,100},{6,102},{8,104},{10,106},{12,108},{14,110},{... | collective-permute-start | bytes 589832 | tf_op jit(solution)/shard_map/ppermute | solution.py:189
  25.0 0.0 collective-permute-done.3.after_ref.refs_4_
  25.0 6.3 %shard_map.50 = (bf16[50,100,1024]{2,1,0:T(8,128)(2,1)S(1)}, bf16[50,100,768]{2,1,0:T(8,128)(2,1)S(1)}, bf16[8,768]{1,0:T(8,128)(2,1)S(1)}) custom-call(bf16[16,8,768]{2,1,0:T(8,128)(2,1)S(1)} %collective-permute-done.3.after_ref.refs_4_, bf16[50,100,1024]{2,1,0:T(8,128)(2,1)} %bitcast.6, bf16[50,100,768]{2,1,0:T(8,128)(2,1)} %bitcast.7), custom_call_target="tpu_custom_call" | custom-call | bytes 17920000 | tf_op jit(solution)/shard_map/pallas_call | solution.py:84
  31.3 0.0 collective-permute-done.2.refs_3_
  31.4 0.0 collective-permute-done.1.refs_2_
  31.4 0.0 collective-permute-done.refs_1_
  31.4 0.1 collective-permute-start.4
  31.5 0.5 collective-permute-start.5
  32.0 0.1 collective-permute-start.6
  32.1 0.8 %collective-permute-done.4.refs_5_ = bf16[16,8,768]{2,1,0:T(8,128)(2,1)S(1)} collective-permute-done((bf16[16,8,768]{2,1,0:T(8,128)(2,1)S(1)}, bf16[16,8,768]{2,1,0:T(8,128)(2,1)S(1)}, u32[]{:S(2)}, u32[]{:S(2)}) %collective-permute-start.4) | collective-permute-done | bytes 196640 | tf_op jit(solution)/shard_map/ppermute | solution.py:187
  32.9 0.3 collective-permute-done.5.refs_6_
  33.2 0.3 collective-permute-done.6.refs_7_
  33.5 11.3 %shard_map.51 = (bf16[50,100,768]{2,1,0:T(8,128)(2,1)}, f32[1,768]{1,0:T(1,128)S(1)}) custom-call(s32[3]{0:T(128)S(1)} %pad_add_fusion.place_ref, bf16[16,8,768]{2,1,0:T(8,128)(2,1)S(1)} %all_to_all.10.refs_0_, bf16[16,8,768]{2,1,0:T(8,128)(2,1)S(1)} %collective-permute-done.refs_1_, bf16[16,8,768]{2,1,0:T(8,128)(2,1)S(1)} %collective-permute-done.1.refs_2_, ...), custom_call_target="tpu_custom_call" | custom-call | flops 7864320000 | bytes 25600000 | tf_op jit(solution)/shard_map/pallas_call | solution.py:150
  44.7 0.3 collective-permute-start.7
  45.0 0.9 %collective-permute-done.7 = f32[1,768]{1,0:T(1,128)S(1)} collective-permute-done((f32[1,768]{1,0:T(1,128)S(1)}, f32[1,768]{1,0:T(1,128)S(1)}, u32[]{:S(2)}, u32[]{:S(2)}) %collective-permute-start.7) | collective-permute-done | bytes 3104 | tf_op jit(solution)/shard_map/ppermute | solution.py:198
  46.0 0.1 broadcast_in_dim.24
  46.1 15.1 %all_to_all.11 = f32[64,1,768]{2,1,0:T(1,128)S(1)} all-to-all(f32[64,1,768]{2,1,0:T(1,128)S(1)} %broadcast_in_dim.24), channel_id=1, replica_groups=mesh['x'=4,'zh'=2,'zl'=2,'y'=4,'c'=2] {'x','zh','zl','y'}, dimensions={0} | all-to-all | bytes 393216 | tf_op jit(solution)/shard_map/all_to_all | solution.py:45
  61.2 0.1 reduce_sum.9
  61.3 0.6 broadcast_multiply_fusion
  (2 shorter events, 0.0 us)
Async XLA Ops:
  19.8 5.2 %collective-permute-start.3 = (bf16[16,8,768]{2,1,0:T(8,128)(2,1)S(1)}, bf16[16,8,768]{2,1,0:T(8,128)(2,1)S(1)}, u32[]{:S(2)}, u32[]{:S(2)}) collective-permute-start(bf16[16,8,768]{2,1,0:T(8,128)(2,1)S(1)} %all_to_all.10.refs_0_), channel_id=1, source_target_pairs={{0,1},{1,0},{2,3},{3,2},{4,5},{5,4},{6,7},{7,6},{8,9},{9,8},{10,11... | collective-permute-start | bytes 589832 | tf_op jit(solution)/shard_map/ppermute | solution.py:187
  19.8 11.5 %collective-permute-start.2 = (bf16[16,8,768]{2,1,0:T(8,128)(2,1)S(1)}, bf16[16,8,768]{2,1,0:T(8,128)(2,1)S(1)}, u32[]{:S(2)}, u32[]{:S(2)}) collective-permute-start(bf16[16,8,768]{2,1,0:T(8,128)(2,1)S(1)} %all_to_all.10.refs_0_), channel_id=1, source_target_pairs={{0,32},{2,34},{4,36},{6,38},{8,40},{10,42},{12,44},{14,46},{16,48}... | collective-permute-start | bytes 589832 | tf_op jit(solution)/shard_map/ppermute | solution.py:190
  21.1 10.2 %collective-permute-start.1 = (bf16[16,8,768]{2,1,0:T(8,128)(2,1)S(1)}, bf16[16,8,768]{2,1,0:T(8,128)(2,1)S(1)}, u32[]{:S(2)}, u32[]{:S(2)}) collective-permute-start(bf16[16,8,768]{2,1,0:T(8,128)(2,1)S(1)} %all_to_all.10.refs_0_), channel_id=1, source_target_pairs={{0,64},{2,66},{4,68},{6,70},{8,72},{10,74},{12,76},{14,78},{16,80}... | collective-permute-start | bytes 589832 | tf_op jit(solution)/shard_map/ppermute | solution.py:188
  23.7 7.7 %collective-permute-start = (bf16[16,8,768]{2,1,0:T(8,128)(2,1)S(1)}, bf16[16,8,768]{2,1,0:T(8,128)(2,1)S(1)}, u32[]{:S(2)}, u32[]{:S(2)}) collective-permute-start(bf16[16,8,768]{2,1,0:T(8,128)(2,1)S(1)} %all_to_all.10.refs_0_), channel_id=1, source_target_pairs={{0,96},{2,98},{4,100},{6,102},{8,104},{10,106},{12,108},{14,110},{... | collective-permute-start | bytes 589832 | tf_op jit(solution)/shard_map/ppermute | solution.py:189
  31.4 1.5 %collective-permute-start.4 = (bf16[16,8,768]{2,1,0:T(8,128)(2,1)S(1)}, bf16[16,8,768]{2,1,0:T(8,128)(2,1)S(1)}, u32[]{:S(2)}, u32[]{:S(2)}) collective-permute-start(bf16[16,8,768]{2,1,0:T(8,128)(2,1)S(1)} %collective-permute-done.refs_1_), channel_id=1, source_target_pairs={{0,1},{1,0},{2,3},{3,2},{4,5},{5,4},{6,7},{7,6},{8,9},{9,8},{10,11... | collective-permute-start | bytes 589832 | tf_op jit(solution)/shard_map/ppermute | solution.py:187
  31.5 1.7 %collective-permute-start.5 = (bf16[16,8,768]{2,1,0:T(8,128)(2,1)S(1)}, bf16[16,8,768]{2,1,0:T(8,128)(2,1)S(1)}, u32[]{:S(2)}, u32[]{:S(2)}) collective-permute-start(bf16[16,8,768]{2,1,0:T(8,128)(2,1)S(1)} %collective-permute-done.1.refs_2_), channel_id=1, source_target_pairs={{0,1},{1,0},{2,3},{3,2},{4,5},{5,4},{6,7},{7,6},{8,9},{9,8},{10,11... | collective-permute-start | bytes 589832 | tf_op jit(solution)/shard_map/ppermute | solution.py:187
  32.0 1.5 %collective-permute-start.6 = (bf16[16,8,768]{2,1,0:T(8,128)(2,1)S(1)}, bf16[16,8,768]{2,1,0:T(8,128)(2,1)S(1)}, u32[]{:S(2)}, u32[]{:S(2)}) collective-permute-start(bf16[16,8,768]{2,1,0:T(8,128)(2,1)S(1)} %collective-permute-done.2.refs_3_), channel_id=1, source_target_pairs={{0,1},{1,0},{2,3},{3,2},{4,5},{5,4},{6,7},{7,6},{8,9},{9,8},{10,11... | collective-permute-start | bytes 589832 | tf_op jit(solution)/shard_map/ppermute | solution.py:187
  44.7 1.2 %collective-permute-start.7 = (f32[1,768]{1,0:T(1,128)S(1)}, f32[1,768]{1,0:T(1,128)S(1)}, u32[]{:S(2)}, u32[]{:S(2)}) collective-permute-start(f32[1,768]{1,0:T(1,128)S(1)} %get-tuple-element.23), channel_id=1, source_target_pairs={{0,1},{1,0},{2,3},{3,2},{4,5},{5,4},{6,7},{7,6},{8,9},{9,8},{10,11... | collective-permute-start | bytes 9224 | tf_op jit(solution)/shard_map/ppermute | solution.py:198

commit v4 on v3

--- a/solution.py
+++ b/solution.py
@@ -36,7 +36,9 @@
 
 LAST_COLS = 10
 LANES = 256
-FETCH_VMEM = 4 << 20
+EARLY = 30
+FETCH_VMEM = 24 << 20
+SPREAD_VMEM = 2 << 20
 LAST_VMEM = 16 << 20
 
 
@@ -68,37 +70,80 @@
 SMEM_SPEC = pl.BlockSpec(memory_space=pltpu.SMEM)
 
 
-def fetch_kernel(after_ref, ints_ref, amps_ref, ints_out, amps_out, token_out, sems):
-    token_out[...] = after_ref[0]
+def fetch_kernel(
+    after_ref, ints_ref, amps_ref, early_ints, early_amps, weights_out, token_out, late_ints, late_amps, sems
+):
+    blocks = ints_ref.shape[0]
+    late, early = pl.ds(EARLY, blocks - EARLY), pl.ds(0, EARLY)
     copies = [
-        pltpu.make_async_copy(ints_ref, ints_out, sems.at[0]),
-        pltpu.make_async_copy(amps_ref, amps_out, sems.at[1]),
+        pltpu.make_async_copy(ints_ref.at[late], late_ints, sems.at[0]),
+        pltpu.make_async_copy(amps_ref.at[late], late_amps, sems.at[1]),
+        pltpu.make_async_copy(ints_ref.at[early], early_ints, sems.at[2]),
+        pltpu.make_async_copy(amps_ref.at[early], early_amps, sems.at[3]),
     ]
     for copy in copies:
         copy.start()
-    for copy in copies:
-        copy.wait()
+    token_out[...] = after_ref[0]
+    copies[0].wait()
+    copies[1].wait()
+    for n in range((blocks - EARLY) // LAST_COLS):
+        span = pl.ds(n * LAST_COLS, LAST_COLS)
+        term = lax.dot_general(
+            padded_rows(late_ints.at[span], LAST_COLS),
+            padded_rows(late_amps.at[span], LAST_COLS),
+            (((0,), (0,)), ((), ())),
+            preferred_element_type=jnp.float32,
+        )
+        weights_out[...] = term if n == 0 else weights_out[...] + term
+    copies[2].wait()
+    copies[3].wait()
 
 
 def fetch(after, ints, amps):
+    late = ints.shape[0] - EARLY
+    kept = (
+        pltpu.VMEM((EARLY, *ints.shape[1:]), ints.dtype),
+        pltpu.VMEM((EARLY, *amps.shape[1:]), amps.dtype),
+    )
     return pl.pallas_call(
         fetch_kernel,
-        out_shape=tuple(pltpu.VMEM(a.shape, a.dtype) for a in (ints, amps, after[0])),
+        out_shape=kept
+        + (pltpu.VMEM((ints.shape[2], amps.shape[2]), jnp.float32), pltpu.VMEM(after.shape[1:], after.dtype)),
         in_specs=[VMEM_SPEC, HBM_SPEC, HBM_SPEC],
-        out_specs=(VMEM_SPEC, VMEM_SPEC, VMEM_SPEC),
-        scratch_shapes=[pltpu.SemaphoreType.DMA((2,))],
+        out_specs=(VMEM_SPEC,) * 4,
+        scratch_shapes=[
+            pltpu.VMEM((late, *ints.shape[1:]), ints.dtype),
+            pltpu.VMEM((late, *amps.shape[1:]), amps.dtype),
+            pltpu.SemaphoreType.DMA((4,)),
+        ],
         compiler_params=pltpu.CompilerParams(vmem_limit_bytes=FETCH_VMEM),
         cost_estimate=pl.CostEstimate(
-            flops=0, bytes_accessed=2 * (ints.size + amps.size), transcendentals=0
+            flops=2 * late * ints.shape[1] * ints.shape[2] * amps.shape[2],
+            bytes_accessed=2 * (ints.size + amps.size),
+            transcendentals=0,
         ),
-    )(after, *(pltpu.with_memory_space_constraint(a, pltpu.HBM) for a in (ints, amps)))
-
-
-def ladder_kernel(place_ref, *refs):
+    )(after, ints, amps)
+
+
+def columns_times(ints_ref, cols_ref, start, nb, done):
+    window, pairs = ints_ref.shape[2], cols_ref.shape[-1]
+    lhs = padded_rows(ints_ref.at[pl.ds(start, nb)], nb)
+    cols = cols_ref[...].reshape(window, pairs)
+    for at in range(0, pairs, LANES):
+        cut = slice(at, at + LANES)
+        total = jnp.dot(lhs, cols[:, cut], preferred_element_type=jnp.float32)
+        done(cut, total.reshape(nb, -1, LANES))
+
+
+def early_kernel(place_ref, *refs):
     mine, theirs = refs[:RING], refs[RING : 2 * RING]
-    ints_ref, amps_ref, _, res_ref, energy_ref, cols_ref, part_ref = refs[2 * RING :]
+    ints_ref, amps_ref, weights_ref, _ = refs[2 * RING : 2 * RING + 4]
+    res_ref, energy_ref, cols_ref, part_ref = refs[2 * RING + 4 :]
     x, z, core = place_ref[0], place_ref[1], place_ref[2]
+    _, rows, window = ints_ref.shape
     pairs = amps_ref.shape[2]
+    nb = LAST_COLS
+    whole = rows // 8 * 8
 
     def put(of_core_0, of_core_1):
         for turn in range(RING):
@@ -115,18 +160,16 @@
         put(theirs, mine)
 
     part_ref[...] = jnp.zeros_like(part_ref)
-    blocks, rows, window = ints_ref.shape
-    nb = LAST_COLS
-    whole = rows // 8 * 8
+    per_x = window // RING
+    for at in range(RING):
+        of_x = cols_ref[at].reshape(per_x, pairs).astype(jnp.float32)
+        product = of_x * weights_ref[at * per_x : (at + 1) * per_x]
+        part_ref[...] += jnp.sum(product.reshape(per_x // 8, 8, pairs), 0)
 
     def body(out_ref):
         start = pl.program_id(0) * nb
-        lhs = padded_rows(ints_ref.at[pl.ds(start, nb)], nb)
-        cols = cols_ref[...].reshape(window, pairs)
-        for at in range(0, pairs, LANES):
-            cut = slice(at, at + LANES)
-            total = jnp.dot(lhs, cols[:, cut], preferred_element_type=jnp.float32)
-            total = total.reshape(nb, -1, LANES)
+
+        def done(cut, total):
             for j in range(nb):
                 full = total[j, :rows]
                 out_ref[j, :, cut] = full.astype(jnp.bfloat16)
@@ -135,37 +178,88 @@
                 if rows > whole:
                     part_ref[: rows - whole, cut] += product[whole:]
 
+        columns_times(ints_ref, cols_ref, start, nb, done)
+
     pltpu.emit_pipeline(
         body,
-        grid=(blocks // nb,),
+        grid=(EARLY // nb,),
         in_specs=[],
         out_specs=[pl.BlockSpec((nb, rows, pairs), lambda s: (s, 0, 0))],
     )(res_ref)
     energy_ref[...] = jnp.sum(part_ref[...], 0, keepdims=True)
 
 
-def ladder(place, mine, theirs, ints, amps, token):
-    blocks, rows, window = ints.shape
+def late_kernel(cols_ref, ints_ref, _, res_ref):
+    blocks, rows, window = ints_ref.shape
+    nb = LAST_COLS
+    first = EARLY // nb
+
+    def body(block_ref, out_ref):
+        def done(cut, total):
+            for j in range(nb):
+                out_ref[j, :, cut] = total[j, :rows].astype(jnp.bfloat16)
+
+        columns_times(block_ref, cols_ref, 0, nb, done)
+
+    pltpu.emit_pipeline(
+        body,
+        grid=((blocks - EARLY) // nb,),
+        in_specs=[pl.BlockSpec((nb, rows, window), lambda s: (s + first, 0, 0))],
+        out_specs=[pl.BlockSpec((nb, rows, cols_ref.shape[-1]), lambda s: (s + first, 0, 0))],
+    )(ints_ref, res_ref)
+
+
+def early_columns(place, mine, theirs, ints, amps, weights, token, blocks):
+    _, rows, window = ints.shape
     pairs = amps.shape[2]
     return pl.pallas_call(
-        ladder_kernel,
+        early_kernel,
         out_shape=(
-            jax.ShapeDtypeStruct(amps.shape, jnp.bfloat16),
-            jax.ShapeDtypeStruct((1, pairs), jnp.float32),
+            jax.ShapeDtypeStruct((blocks, *amps.shape[1:]), jnp.bfloat16),
+            pltpu.VMEM((1, pairs), jnp.float32),
+            pltpu.VMEM((RING, RING, RING, 2, *mine[0].shape[1:]), mine[0].dtype),
         ),
-        in_specs=[SMEM_SPEC] + [VMEM_SPEC] * (2 * RING + 3),
-        out_specs=(HBM_SPEC, VMEM_SPEC),
-        scratch_shapes=[
-            pltpu.VMEM((RING, RING, RING, 2, *mine[0].shape[1:]), mine[0].dtype),
-            pltpu.VMEM((8, pairs), jnp.float32),
-        ],
+        in_specs=[SMEM_SPEC] + [VMEM_SPEC] * (2 * RING + 4),
+        out_specs=(HBM_SPEC, VMEM_SPEC, VMEM_SPEC),
+        scratch_shapes=[pltpu.VMEM((8, pairs), jnp.float32)],
         compiler_params=pltpu.CompilerParams(vmem_limit_bytes=LAST_VMEM),
         cost_estimate=pl.CostEstimate(
-            flops=2 * blocks * rows * window * pairs,
-            bytes_accessed=2 * blocks * rows * (window + 2 * pairs),
+            flops=2 * EARLY * rows * window * pairs, bytes_accessed=2 * EARLY * rows * pairs, transcendentals=0
+        ),
+    )(place, *mine, *theirs, ints, amps, weights, token)
+
+
+def late_columns(cols, ints, residual):
+    blocks, rows, window = ints.shape
+    pairs = residual.shape[2]
+    late = blocks - EARLY
+    return pl.pallas_call(
+        late_kernel,
+        out_shape=jax.ShapeDtypeStruct(residual.shape, residual.dtype),
+        in_specs=[VMEM_SPEC, HBM_SPEC, HBM_SPEC],
+        out_specs=HBM_SPEC,
+        input_output_aliases={2: 0},
+        compiler_params=pltpu.CompilerParams(vmem_limit_bytes=LAST_VMEM),
+        cost_estimate=pl.CostEstimate(
+            flops=2 * late * rows * window * pairs,
+            bytes_accessed=2 * late * rows * (window + pairs),
             transcendentals=0,
         ),
-    )(place, *mine, *theirs, ints, amps, token)
+    )(cols, ints, residual)
+
+
+def spread_kernel(mine_ref, theirs_ref, out_ref):
+    out_ref[...] = jnp.broadcast_to((mine_ref[...] + theirs_ref[...])[None], out_ref.shape)
+
+
+def spread(mine, theirs, copies):
+    return pl.pallas_call(
+        spread_kernel,
+        out_shape=jax.ShapeDtypeStruct((copies, *mine.shape), mine.dtype),
+        in_specs=[VMEM_SPEC, VMEM_SPEC],
+        out_specs=VMEM_SPEC,
+        compiler_params=pltpu.CompilerParams(vmem_limit_bytes=SPREAD_VMEM),
+    )(mine, theirs)
 
 
 def shards(amplitudes, integrals, window_index):
@@ -189,14 +283,18 @@
     above = lax.ppermute(plane, AXES, turned(-1))
     below = lax.ppermute(plane, AXES, turned(1))
     there = swapped(plane)
-    ints, amps, token = fetch(there, ints, amps)
+    ints, amps = (pltpu.with_memory_space_constraint(a, pltpu.HBM) for a in (ints, amps))
+    early_ints, early_amps, weights, token = fetch(there, ints, amps)
     above, across, below, token = lax.optimization_barrier((above, across, below, token))
     mine = (plane, above, across, below)
     theirs = (there, swapped(above), swapped(across), swapped(below))
-    residual, energy = ladder(place, mine, theirs, ints, amps, token)
-
-    chip = energy + lax.ppermute(energy, "c", SWAP)
-    total_energy = jnp.sum(share(chip, CHIPS), axis=(0, 1))
+    residual, energy, cols = early_columns(
+        place, mine, theirs, early_ints, early_amps, weights, token, block_cols
+    )
+
+    chips = spread(energy, swapped(energy), lax.axis_size(CHIPS))
+    total_energy = jnp.sum(lax.all_to_all(chips, CHIPS, 0, 0, tiled=True), axis=(0, 1))
+    residual = late_columns(cols, ints, residual)
     return residual.transpose(1, 0, 2), total_energy / virtuals
 
 

time: 62.2 us -> 60.9 us (0.979)
  blocking collectives: 32 us -> 16.9 us
  Pallas kernels: 17.6 us -> 22.7 us
  starting transfers between devices: 6.16 us -> 11.2 us
  waiting for transfers between devices: 2.35 us -> 6.16 us
    all_to_all x2 -> x1, blocking collectives: 32 us -> 16.9 us  [share(): lax.all_to_all(jnp.broadcast_to(array[None], (devices, *array.shape)), ax...]
    pallas_call x2 -> x4, Pallas kernels: 17.6 us -> 22.7 us  [the longest x1 8.01 us: early_columns(): pl.pallas_call(early_kernel, out_shape=(jax.ShapeDtypeStruct((blocks, *am...]
    all_to_all x0 -> x1, starting transfers between devices: none -> 5.04 us  [shards(): lax.all_to_all(chips, CHIPS, 0, 0, tiled=True)]
    all_to_all x0 -> x1, waiting for transfers between devices: none -> 3.81 us  [shards(): lax.all_to_all(chips, CHIPS, 0, 0, tiled=True)]
    ppermute x4 -> x5, waiting for transfers between devices: 1.4 us -> 2.34 us  [shards(): swapped = lambda array: lax.ppermute(array, 'c', SWAP)]
    ppermute x1 -> x0, waiting for transfers between devices: 0.94 us -> none  [shards(): chip = energy + lax.ppermute(energy, 'c', SWAP)]
  transfers between devices with their start and end apart: 8 -> 9, of which waited for: 4 -> 5; matrix products, arithmetic and copies ran while one was open for 0% -> 0% of each run, Pallas kernels for 10% -> 23%
where the time goes in v4:
time: 60.9 us; the launch traced here: 60.7 us
  Pallas kernels  22.7 us (37%)
  blocking collectives  16.9 us (28%)
  starting transfers between devices  11.2 us (18%)
  waiting for transfers between devices  6.16 us (10%)
  other arithmetic  1.61 us (3%)
  local copies, waits for them, and re-layouts  1.38 us (2%)
  between operations  0.71 us (1%)
    all_to_all x1, blocking collectives, share(): lax.all_to_all(jnp.broadcast_to(array[None], (devices, *array.shape)), ax...  16.9 us
    pallas_call x1, Pallas kernels, early_columns(): pl.pallas_call(early_kernel, out_shape=(jax.ShapeDtypeStruct((blocks, *am...  8.01 us
    pallas_call x1, Pallas kernels, fetch(): pl.pallas_call(fetch_kernel, out_shape=kept + (pltpu.VMEM((ints.shape[2],...  7.55 us
    pallas_call x1, Pallas kernels, late_columns(): pl.pallas_call(late_kernel, out_shape=jax.ShapeDtypeStruct(residual.shape...  6.42 us
    all_to_all x1, starting transfers between devices, shards(): lax.all_to_all(chips, CHIPS, 0, 0, tiled=True)  5.04 us
    all_to_all x1, waiting for transfers between devices, shards(): lax.all_to_all(chips, CHIPS, 0, 0, tiled=True)  3.81 us
    ppermute x1, starting transfers between devices, shards(): across = lax.ppermute(plane, AXES, turned(2))  2.53 us
    ppermute x5, waiting for transfers between devices, shards(): swapped = lambda array: lax.ppermute(array, 'c', SWAP)  2.34 us
  transfers between devices with their start and end apart: 9, of which 5 were waited for; matrix products, arithmetic and copies ran while one was open for 0% of the time, Pallas kernels for 23%

profile of v4, /device:TPU:0, one launch (start us, length us, event | category | flops | bytes accessed | tf_op | source)
XLA Modules:
  0.0 60.7 jit_solution(416688226820291178)
XLA Ops:
  0.6 0.8 %fusion.3 = s32[8]{0:T(128)S(1)} fusion(s32[1024]{0:T(1024)} %param.5, s32[]{:T(128)S(6)} %select_n.21, s32[]{:T(128)S(6)} %mul.36, s32[]{:T(128)S(6)} %mul.35), kind=kLoop, calls=%fused_computation.9 | loop fusion | flops 200 | bytes 76 | tf_op jit(solution)/shard_map/concatenate | solution.py:275
  1.4 1.4 %gather_fusion = bf16[8,768]{1,0:T(8,128)(2,1)S(1)} fusion(bf16[100,50,768]{2,0,1:T(8,128)(2,1)} %param.3, s32[8]{0:T(128)S(1)} %fusion.3), kind=kCustom, calls=%fused_computation | custom fusion | bytes 24640 | tf_op jit(solution)/shard_map/gather | solution.py:275
  2.8 0.1 pad_add_fusion.place_ref
  2.9 16.9 %all_to_all.10.refs_0_ = bf16[16,8,768]{2,1,0:T(8,128)(2,1)S(1)} all-to-all(bf16[16,8,768]{2,1,0:T(8,128)(2,1)S(1)} %broadcast_in_dim.14), channel_id=1, replica_groups={{0,2,4,6,8,10,12,14,16,18,20,22,24,26,28,30},{32,34,36,38,40,42,44,46,4..., dimensions={0} | all-to-all | bytes 393216 | tf_op jit(solution)/shard_map/all_to_all | solution.py:47
  19.8 0.0 collective-permute-start.3
  19.8 1.3 %collective-permute-start.2 = (bf16[16,8,768]{2,1,0:T(8,128)(2,1)S(1)}, bf16[16,8,768]{2,1,0:T(8,128)(2,1)S(1)}, u32[]{:S(2)}, u32[]{:S(2)}) collective-permute-start(bf16[16,8,768]{2,1,0:T(8,128)(2,1)S(1)} %all_to_all.10.refs_0_), channel_id=1, source_target_pairs={{0,32},{2,34},{4,36},{6,38},{8,40},{10,42},{12,44},{14,46},{16,48}... | collective-permute-start | bytes 589832 | tf_op jit(solution)/shard_map/ppermute | solution.py:284
  21.1 2.5 %collective-permute-start.1 = (bf16[16,8,768]{2,1,0:T(8,128)(2,1)S(1)}, bf16[16,8,768]{2,1,0:T(8,128)(2,1)S(1)}, u32[]{:S(2)}, u32[]{:S(2)}) collective-permute-start(bf16[16,8,768]{2,1,0:T(8,128)(2,1)S(1)} %all_to_all.10.refs_0_), channel_id=1, source_target_pairs={{0,64},{2,66},{4,68},{6,70},{8,72},{10,74},{12,76},{14,78},{16,80}... | collective-permute-start | bytes 589832 | tf_op jit(solution)/shard_map/ppermute | solution.py:282
  23.7 1.4 %collective-permute-start = (bf16[16,8,768]{2,1,0:T(8,128)(2,1)S(1)}, bf16[16,8,768]{2,1,0:T(8,128)(2,1)S(1)}, u32[]{:S(2)}, u32[]{:S(2)}) collective-permute-start(bf16[16,8,768]{2,1,0:T(8,128)(2,1)S(1)} %all_to_all.10.refs_0_), channel_id=1, source_target_pairs={{0,96},{2,98},{4,100},{6,102},{8,104},{10,106},{12,108},{14,110},{... | collective-permute-start | bytes 589832 | tf_op jit(solution)/shard_map/ppermute | solution.py:283
  25.0 0.0 collective-permute-done.3.after_ref.refs_4_
  25.0 7.6 %shard_map.50 = (bf16[30,100,1024]{2,1,0:T(8,128)(2,1)S(1)}, bf16[30,100,768]{2,1,0:T(8,128)(2,1)S(1)}, f32[1024,768]{1,0:T(8,128)S(1)}, bf16[8,768]{1,0:T(8,128)(2,1)S(1)}) custom-call(bf16[16,8,768]{2,1,0:T(8,128)(2,1)S(1)} %collective-permute-done.3.after_ref.refs_4_, bf16[50,100,1024]{2,1,0:T(8,128)(2,1)} %bitcast.6, bf16[50,100,768]{2,1,0:T(8,128)(2,1)} %bitcast.8), custom_call_target="tpu_custom_call" | custom-call | flops 3145728000 | bytes 17920000 | tf_op jit(solution)/shard_map/pallas_call | solution.py:108
  32.6 0.0 collective-permute-done.2.refs_3_
  32.6 0.0 collective-permute-done.1.refs_2_
  32.6 0.0 collective-permute-done.refs_1_
  32.6 0.1 collective-permute-start.4
  32.7 0.5 collective-permute-start.5
  33.2 0.1 collective-permute-start.6
  33.3 0.8 %collective-permute-done.4.refs_5_ = bf16[16,8,768]{2,1,0:T(8,128)(2,1)S(1)} collective-permute-done((bf16[16,8,768]{2,1,0:T(8,128)(2,1)S(1)}, bf16[16,8,768]{2,1,0:T(8,128)(2,1)S(1)}, u32[]{:S(2)}, u32[]{:S(2)}) %collective-permute-start.4) | collective-permute-done | bytes 196640 | tf_op jit(solution)/shard_map/ppermute | solution.py:281
  34.1 0.3 collective-permute-done.5.refs_6_
  34.4 0.3 collective-permute-done.6.refs_7_
  34.7 8.0 %shard_map.51 = (bf16[50,100,768]{2,1,0:T(8,128)(2,1)}, f32[1,768]{1,0:T(1,128)S(1)}, bf16[4,4,4,2,8,768]{5,4,3,2,1,0:T(8,128)(2,1)S(1)}) custom-call(s32[3]{0:T(128)S(1)} %pad_add_fusion.place_ref, bf16[16,8,768]{2,1,0:T(8,128)(2,1)S(1)} %all_to_all.10.refs_0_, bf16[16,8,768]{2,1,0:T(8,128)(2,1)S(1)} %collective-permute-done.refs_1_, ...), custom_call_target="tpu_custom_call" | custom-call | flops 4718592000 | bytes 4608000 | tf_op jit(solution)/shard_map/pallas_call | solution.py:215
  42.7 0.3 collective-permute-start.7
  43.0 0.9 %collective-permute-done.7.theirs_ref = f32[1,768]{1,0:T(1,128)S(1)} collective-permute-done((f32[1,768]{1,0:T(1,128)S(1)}, f32[1,768]{1,0:T(1,128)S(1)}, u32[]{:S(2)}, u32[]{:S(2)}) %collective-permute-start.7) | collective-permute-done | bytes 3104 | tf_op jit(solution)/shard_map/ppermute | solution.py:281
  44.0 0.7 %shard_map.53 = f32[64,1,768]{2,1,0:T(1,128)} custom-call(f32[1,768]{1,0:T(1,128)S(1)} %get-tuple-element.27.mine_ref, f32[1,768]{1,0:T(1,128)S(1)} %collective-permute-done.7.theirs_ref), custom_call_target="tpu_custom_call" | custom-call | tf_op jit(solution)/shard_map/pallas_call | solution.py:256
  44.7 5.0 %all-to-all-start.1 = ((f32[64,1,768]{2,1,0:T(1,128)}), f32[64,1,768]{2,1,0:T(1,128)S(1)}, u32[]{:S(2)}, u32[]{:S(2)}) async-start(f32[64,1,768]{2,1,0:T(1,128)} %shard_map.53), calls=%async_computation.1 | async-start | bytes 393216 | tf_op jit(solution)/shard_map/all_to_all | solution.py:296
  49.7 6.4 %shard_map.52 = bf16[50,100,768]{2,1,0:T(8,128)(2,1)} custom-call(bf16[4,4,4,2,8,768]{5,4,3,2,1,0:T(8,128)(2,1)S(1)} %get-tuple-element.25.cols_ref, bf16[50,100,1024]{2,1,0:T(8,128)(2,1)} %bitcast.7, bf16[50,100,768]{2,1,0:T(8,128)(2,1)} %get-tuple-element.26._), custom_call_target="tpu_custom_call", output_to_operand_aliasing={{}: (2, {})} | custom-call | flops 3145728000 | bytes 7168000 | tf_op jit(solution)/shard_map/pallas_call | solution.py:236
  56.1 3.8 %all-to-all-done.1 = f32[64,1,768]{2,1,0:T(1,128)S(1)} async-done(((f32[64,1,768]{2,1,0:T(1,128)}), f32[64,1,768]{2,1,0:T(1,128)S(1)}, u32[]{:S(2)}, u32[]{:S(2)}) %all-to-all-start.1) | async-done | bytes 196640 | tf_op jit(solution)/shard_map/all_to_all | solution.py:296
  59.9 0.1 reduce_sum.9
  60.1 0.6 broadcast_multiply_fusion
  (1 shorter events, 0.0 us)
Async XLA Ops:
  19.8 5.2 %collective-permute-start.3 = (bf16[16,8,768]{2,1,0:T(8,128)(2,1)S(1)}, bf16[16,8,768]{2,1,0:T(8,128)(2,1)S(1)}, u32[]{:S(2)}, u32[]{:S(2)}) collective-permute-start(bf16[16,8,768]{2,1,0:T(8,128)(2,1)S(1)} %all_to_all.10.refs_0_), channel_id=1, source_target_pairs={{0,1},{1,0},{2,3},{3,2},{4,5},{5,4},{6,7},{7,6},{8,9},{9,8},{10,11... | collective-permute-start | bytes 589832 | tf_op jit(solution)/shard_map/ppermute | solution.py:281
  19.8 12.8 %collective-permute-start.2 = (bf16[16,8,768]{2,1,0:T(8,128)(2,1)S(1)}, bf16[16,8,768]{2,1,0:T(8,128)(2,1)S(1)}, u32[]{:S(2)}, u32[]{:S(2)}) collective-permute-start(bf16[16,8,768]{2,1,0:T(8,128)(2,1)S(1)} %all_to_all.10.refs_0_), channel_id=1, source_target_pairs={{0,32},{2,34},{4,36},{6,38},{8,40},{10,42},{12,44},{14,46},{16,48}... | collective-permute-start | bytes 589832 | tf_op jit(solution)/shard_map/ppermute | solution.py:284
  21.1 11.5 %collective-permute-start.1 = (bf16[16,8,768]{2,1,0:T(8,128)(2,1)S(1)}, bf16[16,8,768]{2,1,0:T(8,128)(2,1)S(1)}, u32[]{:S(2)}, u32[]{:S(2)}) collective-permute-start(bf16[16,8,768]{2,1,0:T(8,128)(2,1)S(1)} %all_to_all.10.refs_0_), channel_id=1, source_target_pairs={{0,64},{2,66},{4,68},{6,70},{8,72},{10,74},{12,76},{14,78},{16,80}... | collective-permute-start | bytes 589832 | tf_op jit(solution)/shard_map/ppermute | solution.py:282
  23.7 8.9 %collective-permute-start = (bf16[16,8,768]{2,1,0:T(8,128)(2,1)S(1)}, bf16[16,8,768]{2,1,0:T(8,128)(2,1)S(1)}, u32[]{:S(2)}, u32[]{:S(2)}) collective-permute-start(bf16[16,8,768]{2,1,0:T(8,128)(2,1)S(1)} %all_to_all.10.refs_0_), channel_id=1, source_target_pairs={{0,96},{2,98},{4,100},{6,102},{8,104},{10,106},{12,108},{14,110},{... | collective-permute-start | bytes 589832 | tf_op jit(solution)/shard_map/ppermute | solution.py:283
  32.6 1.5 %collective-permute-start.4 = (bf16[16,8,768]{2,1,0:T(8,128)(2,1)S(1)}, bf16[16,8,768]{2,1,0:T(8,128)(2,1)S(1)}, u32[]{:S(2)}, u32[]{:S(2)}) collective-permute-start(bf16[16,8,768]{2,1,0:T(8,128)(2,1)S(1)} %collective-permute-done.refs_1_), channel_id=1, source_target_pairs={{0,1},{1,0},{2,3},{3,2},{4,5},{5,4},{6,7},{7,6},{8,9},{9,8},{10,11... | collective-permute-start | bytes 589832 | tf_op jit(solution)/shard_map/ppermute | solution.py:281
  32.7 1.7 %collective-permute-start.5 = (bf16[16,8,768]{2,1,0:T(8,128)(2,1)S(1)}, bf16[16,8,768]{2,1,0:T(8,128)(2,1)S(1)}, u32[]{:S(2)}, u32[]{:S(2)}) collective-permute-start(bf16[16,8,768]{2,1,0:T(8,128)(2,1)S(1)} %collective-permute-done.1.refs_2_), channel_id=1, source_target_pairs={{0,1},{1,0},{2,3},{3,2},{4,5},{5,4},{6,7},{7,6},{8,9},{9,8},{10,11... | collective-permute-start | bytes 589832 | tf_op jit(solution)/shard_map/ppermute | solution.py:281
  33.2 1.5 %collective-permute-start.6 = (bf16[16,8,768]{2,1,0:T(8,128)(2,1)S(1)}, bf16[16,8,768]{2,1,0:T(8,128)(2,1)S(1)}, u32[]{:S(2)}, u32[]{:S(2)}) collective-permute-start(bf16[16,8,768]{2,1,0:T(8,128)(2,1)S(1)} %collective-permute-done.2.refs_3_), channel_id=1, source_target_pairs={{0,1},{1,0},{2,3},{3,2},{4,5},{5,4},{6,7},{7,6},{8,9},{9,8},{10,11... | collective-permute-start | bytes 589832 | tf_op jit(solution)/shard_map/ppermute | solution.py:281
  42.7 1.2 %collective-permute-start.7 = (f32[1,768]{1,0:T(1,128)S(1)}, f32[1,768]{1,0:T(1,128)S(1)}, u32[]{:S(2)}, u32[]{:S(2)}) collective-permute-start(f32[1,768]{1,0:T(1,128)S(1)} %get-tuple-element.27.mine_ref), channel_id=1, source_target_pairs={{0,1},{1,0},{2,3},{3,2},{4,5},{5,4},{6,7},{7,6},{8,9},{9,8},{10,11... | collective-permute-start | bytes 9224 | tf_op jit(solution)/shard_map/ppermute | solution.py:281
  44.7 15.3 %all-to-all-start.1 = ((f32[64,1,768]{2,1,0:T(1,128)}), f32[64,1,768]{2,1,0:T(1,128)S(1)}, u32[]{:S(2)}, u32[]{:S(2)}) async-start(f32[64,1,768]{2,1,0:T(1,128)} %shard_map.53), calls=%async_computation.1 | async-start | bytes 393216 | tf_op jit(solution)/shard_map/all_to_all | solution.py:296

commit v5 on v4

--- a/solution.py
+++ b/solution.py
@@ -35,7 +35,7 @@
 
 
 LAST_COLS = 10
-LANES = 256
+LANES = 768
 EARLY = 30
 FETCH_VMEM = 24 << 20
 SPREAD_VMEM = 2 << 20

time: 60.9 us -> 60.9 us (level)
  no operation moved by 1% of the time
where the time goes in v5:
time: 60.9 us; the launch traced here: 60.7 us
  Pallas kernels  22.7 us (37%)
  blocking collectives  16.9 us (28%)
  starting transfers between devices  11.2 us (18%)
  waiting for transfers between devices  6.16 us (10%)
  other arithmetic  1.61 us (3%)
  local copies, waits for them, and re-layouts  1.38 us (2%)
  between operations  0.71 us (1%)
    all_to_all x1, blocking collectives, share(): lax.all_to_all(jnp.broadcast_to(array[None], (devices, *array.shape)), ax...  16.9 us
    pallas_call x1, Pallas kernels, early_columns(): pl.pallas_call(early_kernel, out_shape=(jax.ShapeDtypeStruct((blocks, *am...  8.01 us
    pallas_call x1, Pallas kernels, fetch(): pl.pallas_call(fetch_kernel, out_shape=kept + (pltpu.VMEM((ints.shape[2],...  7.55 us
    pallas_call x1, Pallas kernels, late_columns(): pl.pallas_call(late_kernel, out_shape=jax.ShapeDtypeStruct(residual.shape...  6.42 us
    all_to_all x1, starting transfers between devices, shards(): lax.all_to_all(chips, CHIPS, 0, 0, tiled=True)  5.04 us
    all_to_all x1, waiting for transfers between devices, shards(): lax.all_to_all(chips, CHIPS, 0, 0, tiled=True)  3.81 us
    ppermute x1, starting transfers between devices, shards(): across = lax.ppermute(plane, AXES, turned(2))  2.53 us
    ppermute x5, waiting for transfers between devices, shards(): swapped = lambda array: lax.ppermute(array, 'c', SWAP)  2.34 us
  transfers between devices with their start and end apart: 9, of which 5 were waited for; matrix products, arithmetic and copies ran while one was open for 0% of the time, Pallas kernels for 23%

profile of v5, /device:TPU:0, one launch (start us, length us, event | category | flops | bytes accessed | tf_op | source)
XLA Modules:
  0.0 60.7 jit_solution(416688226820291178)
XLA Ops:
  0.6 0.8 %fusion.3 = s32[8]{0:T(128)S(1)} fusion(s32[1024]{0:T(1024)} %param.5, s32[]{:T(128)S(6)} %select_n.21, s32[]{:T(128)S(6)} %mul.36, s32[]{:T(128)S(6)} %mul.35), kind=kLoop, calls=%fused_computation.9 | loop fusion | flops 200 | bytes 76 | tf_op jit(solution)/shard_map/concatenate | solution.py:275
  1.4 1.4 %gather_fusion = bf16[8,768]{1,0:T(8,128)(2,1)S(1)} fusion(bf16[100,50,768]{2,0,1:T(8,128)(2,1)} %param.3, s32[8]{0:T(128)S(1)} %fusion.3), kind=kCustom, calls=%fused_computation | custom fusion | bytes 24640 | tf_op jit(solution)/shard_map/gather | solution.py:275
  2.8 0.1 pad_add_fusion.place_ref
  2.9 16.9 %all_to_all.10.refs_0_ = bf16[16,8,768]{2,1,0:T(8,128)(2,1)S(1)} all-to-all(bf16[16,8,768]{2,1,0:T(8,128)(2,1)S(1)} %broadcast_in_dim.14), channel_id=1, replica_groups={{0,2,4,6,8,10,12,14,16,18,20,22,24,26,28,30},{32,34,36,38,40,42,44,46,4..., dimensions={0} | all-to-all | bytes 393216 | tf_op jit(solution)/shard_map/all_to_all | solution.py:47
  19.8 0.0 collective-permute-start.3
  19.8 1.3 %collective-permute-start.2 = (bf16[16,8,768]{2,1,0:T(8,128)(2,1)S(1)}, bf16[16,8,768]{2,1,0:T(8,128)(2,1)S(1)}, u32[]{:S(2)}, u32[]{:S(2)}) collective-permute-start(bf16[16,8,768]{2,1,0:T(8,128)(2,1)S(1)} %all_to_all.10.refs_0_), channel_id=1, source_target_pairs={{0,32},{2,34},{4,36},{6,38},{8,40},{10,42},{12,44},{14,46},{16,48}... | collective-permute-start | bytes 589832 | tf_op jit(solution)/shard_map/ppermute | solution.py:284
  21.1 2.5 %collective-permute-start.1 = (bf16[16,8,768]{2,1,0:T(8,128)(2,1)S(1)}, bf16[16,8,768]{2,1,0:T(8,128)(2,1)S(1)}, u32[]{:S(2)}, u32[]{:S(2)}) collective-permute-start(bf16[16,8,768]{2,1,0:T(8,128)(2,1)S(1)} %all_to_all.10.refs_0_), channel_id=1, source_target_pairs={{0,64},{2,66},{4,68},{6,70},{8,72},{10,74},{12,76},{14,78},{16,80}... | collective-permute-start | bytes 589832 | tf_op jit(solution)/shard_map/ppermute | solution.py:282
  23.7 1.4 %collective-permute-start = (bf16[16,8,768]{2,1,0:T(8,128)(2,1)S(1)}, bf16[16,8,768]{2,1,0:T(8,128)(2,1)S(1)}, u32[]{:S(2)}, u32[]{:S(2)}) collective-permute-start(bf16[16,8,768]{2,1,0:T(8,128)(2,1)S(1)} %all_to_all.10.refs_0_), channel_id=1, source_target_pairs={{0,96},{2,98},{4,100},{6,102},{8,104},{10,106},{12,108},{14,110},{... | collective-permute-start | bytes 589832 | tf_op jit(solution)/shard_map/ppermute | solution.py:283
  25.0 0.0 collective-permute-done.3.after_ref.refs_4_
  25.0 7.6 %shard_map.50 = (bf16[30,100,1024]{2,1,0:T(8,128)(2,1)S(1)}, bf16[30,100,768]{2,1,0:T(8,128)(2,1)S(1)}, f32[1024,768]{1,0:T(8,128)S(1)}, bf16[8,768]{1,0:T(8,128)(2,1)S(1)}) custom-call(bf16[16,8,768]{2,1,0:T(8,128)(2,1)S(1)} %collective-permute-done.3.after_ref.refs_4_, bf16[50,100,1024]{2,1,0:T(8,128)(2,1)} %bitcast.6, bf16[50,100,768]{2,1,0:T(8,128)(2,1)} %bitcast.8), custom_call_target="tpu_custom_call" | custom-call | flops 3145728000 | bytes 17920000 | tf_op jit(solution)/shard_map/pallas_call | solution.py:108
  32.6 0.0 collective-permute-done.2.refs_3_
  32.6 0.0 collective-permute-done.1.refs_2_
  32.6 0.0 collective-permute-done.refs_1_
  32.6 0.1 collective-permute-start.4
  32.7 0.5 collective-permute-start.5
  33.2 0.1 collective-permute-start.6
  33.3 0.8 %collective-permute-done.4.refs_5_ = bf16[16,8,768]{2,1,0:T(8,128)(2,1)S(1)} collective-permute-done((bf16[16,8,768]{2,1,0:T(8,128)(2,1)S(1)}, bf16[16,8,768]{2,1,0:T(8,128)(2,1)S(1)}, u32[]{:S(2)}, u32[]{:S(2)}) %collective-permute-start.4) | collective-permute-done | bytes 196640 | tf_op jit(solution)/shard_map/ppermute | solution.py:281
  34.1 0.3 collective-permute-done.5.refs_6_
  34.4 0.3 collective-permute-done.6.refs_7_
  34.7 8.0 %shard_map.51 = (bf16[50,100,768]{2,1,0:T(8,128)(2,1)}, f32[1,768]{1,0:T(1,128)S(1)}, bf16[4,4,4,2,8,768]{5,4,3,2,1,0:T(8,128)(2,1)S(1)}) custom-call(s32[3]{0:T(128)S(1)} %pad_add_fusion.place_ref, bf16[16,8,768]{2,1,0:T(8,128)(2,1)S(1)} %all_to_all.10.refs_0_, bf16[16,8,768]{2,1,0:T(8,128)(2,1)S(1)} %collective-permute-done.refs_1_, ...), custom_call_target="tpu_custom_call" | custom-call | flops 4718592000 | bytes 4608000 | tf_op jit(solution)/shard_map/pallas_call | solution.py:215
  42.7 0.3 collective-permute-start.7
  43.0 0.9 %collective-permute-done.7.theirs_ref = f32[1,768]{1,0:T(1,128)S(1)} collective-permute-done((f32[1,768]{1,0:T(1,128)S(1)}, f32[1,768]{1,0:T(1,128)S(1)}, u32[]{:S(2)}, u32[]{:S(2)}) %collective-permute-start.7) | collective-permute-done | bytes 3104 | tf_op jit(solution)/shard_map/ppermute | solution.py:281
  44.0 0.7 %shard_map.53 = f32[64,1,768]{2,1,0:T(1,128)} custom-call(f32[1,768]{1,0:T(1,128)S(1)} %get-tuple-element.27.mine_ref, f32[1,768]{1,0:T(1,128)S(1)} %collective-permute-done.7.theirs_ref), custom_call_target="tpu_custom_call" | custom-call | tf_op jit(solution)/shard_map/pallas_call | solution.py:256
  44.7 5.0 %all-to-all-start.1 = ((f32[64,1,768]{2,1,0:T(1,128)}), f32[64,1,768]{2,1,0:T(1,128)S(1)}, u32[]{:S(2)}, u32[]{:S(2)}) async-start(f32[64,1,768]{2,1,0:T(1,128)} %shard_map.53), calls=%async_computation.1 | async-start | bytes 393216 | tf_op jit(solution)/shard_map/all_to_all | solution.py:296
  49.7 6.4 %shard_map.52 = bf16[50,100,768]{2,1,0:T(8,128)(2,1)} custom-call(bf16[4,4,4,2,8,768]{5,4,3,2,1,0:T(8,128)(2,1)S(1)} %get-tuple-element.25.cols_ref, bf16[50,100,1024]{2,1,0:T(8,128)(2,1)} %bitcast.7, bf16[50,100,768]{2,1,0:T(8,128)(2,1)} %get-tuple-element.26._), custom_call_target="tpu_custom_call", output_to_operand_aliasing={{}: (2, {})} | custom-call | flops 3145728000 | bytes 7168000 | tf_op jit(solution)/shard_map/pallas_call | solution.py:236
  56.1 3.8 %all-to-all-done.1 = f32[64,1,768]{2,1,0:T(1,128)S(1)} async-done(((f32[64,1,768]{2,1,0:T(1,128)}), f32[64,1,768]{2,1,0:T(1,128)S(1)}, u32[]{:S(2)}, u32[]{:S(2)}) %all-to-all-start.1) | async-done | bytes 196640 | tf_op jit(solution)/shard_map/all_to_all | solution.py:296
  59.9 0.1 reduce_sum.9
  60.1 0.6 broadcast_multiply_fusion
  (1 shorter events, 0.0 us)
Async XLA Ops:
  19.8 5.2 %collective-permute-start.3 = (bf16[16,8,768]{2,1,0:T(8,128)(2,1)S(1)}, bf16[16,8,768]{2,1,0:T(8,128)(2,1)S(1)}, u32[]{:S(2)}, u32[]{:S(2)}) collective-permute-start(bf16[16,8,768]{2,1,0:T(8,128)(2,1)S(1)} %all_to_all.10.refs_0_), channel_id=1, source_target_pairs={{0,1},{1,0},{2,3},{3,2},{4,5},{5,4},{6,7},{7,6},{8,9},{9,8},{10,11... | collective-permute-start | bytes 589832 | tf_op jit(solution)/shard_map/ppermute | solution.py:281
  19.8 12.8 %collective-permute-start.2 = (bf16[16,8,768]{2,1,0:T(8,128)(2,1)S(1)}, bf16[16,8,768]{2,1,0:T(8,128)(2,1)S(1)}, u32[]{:S(2)}, u32[]{:S(2)}) collective-permute-start(bf16[16,8,768]{2,1,0:T(8,128)(2,1)S(1)} %all_to_all.10.refs_0_), channel_id=1, source_target_pairs={{0,32},{2,34},{4,36},{6,38},{8,40},{10,42},{12,44},{14,46},{16,48}... | collective-permute-start | bytes 589832 | tf_op jit(solution)/shard_map/ppermute | solution.py:284
  21.1 11.5 %collective-permute-start.1 = (bf16[16,8,768]{2,1,0:T(8,128)(2,1)S(1)}, bf16[16,8,768]{2,1,0:T(8,128)(2,1)S(1)}, u32[]{:S(2)}, u32[]{:S(2)}) collective-permute-start(bf16[16,8,768]{2,1,0:T(8,128)(2,1)S(1)} %all_to_all.10.refs_0_), channel_id=1, source_target_pairs={{0,64},{2,66},{4,68},{6,70},{8,72},{10,74},{12,76},{14,78},{16,80}... | collective-permute-start | bytes 589832 | tf_op jit(solution)/shard_map/ppermute | solution.py:282
  23.7 8.9 %collective-permute-start = (bf16[16,8,768]{2,1,0:T(8,128)(2,1)S(1)}, bf16[16,8,768]{2,1,0:T(8,128)(2,1)S(1)}, u32[]{:S(2)}, u32[]{:S(2)}) collective-permute-start(bf16[16,8,768]{2,1,0:T(8,128)(2,1)S(1)} %all_to_all.10.refs_0_), channel_id=1, source_target_pairs={{0,96},{2,98},{4,100},{6,102},{8,104},{10,106},{12,108},{14,110},{... | collective-permute-start | bytes 589832 | tf_op jit(solution)/shard_map/ppermute | solution.py:283
  32.6 1.5 %collective-permute-start.4 = (bf16[16,8,768]{2,1,0:T(8,128)(2,1)S(1)}, bf16[16,8,768]{2,1,0:T(8,128)(2,1)S(1)}, u32[]{:S(2)}, u32[]{:S(2)}) collective-permute-start(bf16[16,8,768]{2,1,0:T(8,128)(2,1)S(1)} %collective-permute-done.refs_1_), channel_id=1, source_target_pairs={{0,1},{1,0},{2,3},{3,2},{4,5},{5,4},{6,7},{7,6},{8,9},{9,8},{10,11... | collective-permute-start | bytes 589832 | tf_op jit(solution)/shard_map/ppermute | solution.py:281
  32.7 1.7 %collective-permute-start.5 = (bf16[16,8,768]{2,1,0:T(8,128)(2,1)S(1)}, bf16[16,8,768]{2,1,0:T(8,128)(2,1)S(1)}, u32[]{:S(2)}, u32[]{:S(2)}) collective-permute-start(bf16[16,8,768]{2,1,0:T(8,128)(2,1)S(1)} %collective-permute-done.1.refs_2_), channel_id=1, source_target_pairs={{0,1},{1,0},{2,3},{3,2},{4,5},{5,4},{6,7},{7,6},{8,9},{9,8},{10,11... | collective-permute-start | bytes 589832 | tf_op jit(solution)/shard_map/ppermute | solution.py:281
  33.2 1.5 %collective-permute-start.6 = (bf16[16,8,768]{2,1,0:T(8,128)(2,1)S(1)}, bf16[16,8,768]{2,1,0:T(8,128)(2,1)S(1)}, u32[]{:S(2)}, u32[]{:S(2)}) collective-permute-start(bf16[16,8,768]{2,1,0:T(8,128)(2,1)S(1)} %collective-permute-done.2.refs_3_), channel_id=1, source_target_pairs={{0,1},{1,0},{2,3},{3,2},{4,5},{5,4},{6,7},{7,6},{8,9},{9,8},{10,11... | collective-permute-start | bytes 589832 | tf_op jit(solution)/shard_map/ppermute | solution.py:281
  42.7 1.2 %collective-permute-start.7 = (f32[1,768]{1,0:T(1,128)S(1)}, f32[1,768]{1,0:T(1,128)S(1)}, u32[]{:S(2)}, u32[]{:S(2)}) collective-permute-start(f32[1,768]{1,0:T(1,128)S(1)} %get-tuple-element.27.mine_ref), channel_id=1, source_target_pairs={{0,1},{1,0},{2,3},{3,2},{4,5},{5,4},{6,7},{7,6},{8,9},{9,8},{10,11... | collective-permute-start | bytes 9224 | tf_op jit(solution)/shard_map/ppermute | solution.py:281
  44.7 15.3 %all-to-all-start.1 = ((f32[64,1,768]{2,1,0:T(1,128)}), f32[64,1,768]{2,1,0:T(1,128)S(1)}, u32[]{:S(2)}, u32[]{:S(2)}) async-start(f32[64,1,768]{2,1,0:T(1,128)} %shard_map.53), calls=%async_computation.1 | async-start | bytes 393216 | tf_op jit(solution)/shard_map/all_to_all | solution.py:296
